TPU v7x, 512 devices: a whole 4x4x16 slice. The times are simulated.
512 devices in a mesh: gx: 32 (over y_lo, z), gy: 16 (over x, y_hi, core).
Axes of the slice: x: 4, y: 4 (y_hi: 2, y_lo: 2; y = y_hi * 2 + y_lo), z: 16, core: 2. Of those that a mesh axis runs over, the one named last changes fastest.
Arguments:
- interior_inverse: bfloat16 [32, 16, 768, 768], P('gx', 'gy'), as said below
- coupling: bfloat16 [32, 16, 768, 1024], P('gx', 'gy'), may hold values from -1 to 1
- face_matrix: bfloat16 [32, 16, 4, 256, 256], P('gx', 'gy'), as said below
- face_modes: bfloat16 [32, 16, 256, 128], P('gx', 'gy'), may hold values from -0.125 to 0.125
- face_links: int32 [32, 16, 4], P('gx', 'gy'), may hold values from 0 to 1, as said below
- owner_map: int32 [32, 16, 128], P('gx', 'gy'), may hold values from 0 to 255
Outputs:
- deluxe: float32 [32, 16, 4, 256, 256], P('gx', 'gy')
- coarse_rows: float32 [32, 256, 128], P('gx', 'gy')
Inputs may be any that keep to these rules, and one draw needn't show every extreme that they name: `interior_inverse`: each matrix symmetric positive definite. `face_matrix`: each block symmetric positive definite. `face_links`: face 0 of a subdomain equals face 1 of the subdomain before it along the grid rows, face 2 equals face 3 of the one before it along the columns; faces on the grid's outer boundary are 0.
All inputs are finite; a program needn't handle non-finite values.
Results may differ from a plain program's by a relative error of at most 0.0003.
Values sent between devices are 32-bit elements; how exact they have to be, the bound alone decides.
No kernel may reach another device: no remote copies, remote signals or barrier semaphores. Data moves between devices by JAX's collectives and lax.ppermute only.
A program may use at most 64 MiB of HBM per device.

v0:
```python
import jax
import jax.numpy as jnp
from jax import lax
from jax.sharding import PartitionSpec as P

NF = 256
FACES = 4
MODES = 32
CROWS = 16


def shifted(value, axis, steps):
    count = lax.axis_size(axis)
    initial, last = (max(0, -steps), min(count, count - steps))
    return lax.ppermute(value, axis, [(source, source + steps) for source in range(initial, last)])


def contract_rows(left, right):
    return lax.dot_general(
        left, right, (((0,), (0,)), ((), ())), preferred_element_type=jnp.float32
    )


def contract_exact(left, right):
    return lax.dot_general(left, right, (((0,), (0,)), ((), ())), precision=lax.Precision.HIGHEST)


def face_block(matrix, number, faces):
    lower = number * NF
    gram_block = matrix[lower : lower + NF, lower : lower + NF]
    return faces[number].astype(jnp.float32) - 0.5 * (gram_block + gram_block.T)


def row_partners(north_block, south_block):
    above = shifted(south_block, "gx", 1)
    below = shifted(north_block, "gx", -1)
    return (above, below)


def column_partners(west_block, east_block):
    left_side = shifted(east_block, "gy", 1)
    right_side = shifted(west_block, "gy", -1)
    return (left_side, right_side)


def solve_face(factor_one, right_one):
    return jax.scipy.linalg.cho_solve((factor_one, True), right_one)


def body(interior_inverse, coupling, face_matrix, face_modes, face_links, owner_map):
    inverse = interior_inverse[0, 0]
    couple = coupling[0, 0]
    faces = face_matrix[0, 0]
    modes = face_modes[0, 0]
    links = face_links[0, 0].astype(jnp.float32)
    owners = owner_map[0, 0]
    solved = jnp.dot(inverse, couple, preferred_element_type=jnp.float32).astype(jnp.bfloat16)
    gram_full = contract_rows(couple, solved)
    own_north = face_block(gram_full, 0, faces)
    own_south = face_block(gram_full, 1, faces)
    north_part, south_part = row_partners(own_north, own_south)
    own_west = face_block(gram_full, 2, faces)
    own_east = face_block(gram_full, 3, faces)
    west_part, east_part = column_partners(own_west, own_east)
    own_blocks = jnp.stack([own_north, own_south, own_west, own_east])
    partners = jnp.stack([north_part, south_part, west_part, east_part]) * links[:, None, None]
    factors = jnp.linalg.cholesky(own_blocks + partners)
    deluxe = jax.vmap(solve_face)(factors, own_blocks)
    mapped = [
        jnp.dot(
            deluxe[n],
            modes[:, n * MODES : (n + 1) * MODES].astype(jnp.float32),
            precision=lax.Precision.HIGHEST,
        )
        for n in range(FACES)
    ]
    schur_full = -0.5 * (gram_full + gram_full.T)
    phi_full = jnp.zeros((FACES * NF, FACES * MODES), jnp.float32)
    for number in range(FACES):
        lower = number * NF
        schur_full = schur_full.at[lower : lower + NF, lower : lower + NF].add(
            faces[number].astype(jnp.float32)
        )
        phi_full = phi_full.at[lower : lower + NF, number * MODES : (number + 1) * MODES].set(
            mapped[number]
        )
    product = jnp.dot(schur_full, phi_full, precision=lax.Precision.HIGHEST)
    local = contract_exact(phi_full, product)
    weights = jnp.repeat(links, MODES)
    local = local * weights[:, None] * weights[None, :]
    slots = lax.broadcasted_iota(jnp.int32, (CROWS * lax.axis_size("gy"), 1), 0)
    onehot = (owners[None, :] == slots).astype(jnp.float32)
    coarse = lax.psum_scatter(
        jnp.dot(onehot, local, precision=lax.Precision.HIGHEST),
        "gy",
        scatter_dimension=0,
        tiled=True,
    )
    return (deluxe[None, None], coarse[None])


def solution(mesh):
    placed = (
        P("gx", "gy", None, None),
        P("gx", "gy", None, None),
        P("gx", "gy", None, None, None),
        P("gx", "gy", None, None),
        P("gx", "gy", None),
        P("gx", "gy", None),
    )
    return jax.shard_map(
        body,
        mesh=mesh,
        in_specs=placed,
        out_specs=(P("gx", "gy", None, None, None), P("gx", "gy", None)),
        check_vma=False,
    )
```

profile of v0, /device:TPU:2, one launch (start us, length us, event | category | flops | bytes accessed | tf_op | source)
XLA Modules:
  0.0 403.9 jit_solution(16877992598240630742)
XLA Ops:
  8.7 6.2 %fusion = f32[1024,1024]{1,0:T(8,128)} fusion(bf16[1,1,768,1024]{3,2,1,0:T(8,128)(2,1)S(1)} %copy-done, bf16[1,1,768,768]{3,2,1,0:T(8,128)(2,1)} %param.22), kind=kOutput, calls=%fused_computation.13 | convolution fusion | flops 2819358720 | bytes 6946816 | tf_op jit(solution)/shard_map/dot_general | solution.py:19
  14.9 5.4 %copy.30 = f32[1024,1024]{0,1:T(8,128)} copy(f32[1024,1024]{1,0:T(8,128)} %fusion) | data formatting | bytes 8388608 | tf_op jit(solution)/shard_map/dot_general | solution.py:19
  22.7 1.7 fusion.35
  24.4 4.5 %collective-permute-start.3 = (f32[256,256]{0,1:T(8,128)}, f32[256,256]{0,1:T(8,128)}, u32[]{:S(2)}, u32[]{:S(2)}) collective-permute-start(f32[256,256]{0,1:T(8,128)} %fusion.35), channel_id=1, source_target_pairs={{1,0},{2,1},{3,2},{4,3},{5,4},{6,5},{7,6},{8,7},{9,8},{10,9},{11,1... | collective-permute-start | bytes 786440 | tf_op jit(solution)/shard_map/ppermute | solution.py:15
  29.2 2.1 collective-permute-start.2
  31.3 6.9 %add_multiply_fusion = f32[1024,1024]{1,0:T(8,128)} fusion(f32[1024,1024]{1,0:T(8,128)} %fusion, f32[1024,1024]{0,1:T(8,128)} %copy.30), kind=kLoop, calls=%fused_computation.2 | loop fusion | flops 2097152 | bytes 12582912 | tf_op jit(solution)/shard_map/mul | solution.py:77
  39.5 1.7 fusion.14
  41.2 1.7 fusion.15
  42.9 1.7 fusion.30
  44.7 2.0 convert_subtract_fusion.1
  46.6 1.3 collective-permute-start.1
  47.9 4.6 %collective-permute-start = (f32[256,256]{1,0:T(8,128)S(1)}, f32[256,256]{1,0:T(8,128)S(1)}, u32[]{:S(2)}, u32[]{:S(2)}) collective-permute-start(f32[256,256]{1,0:T(8,128)S(1)} %get-tuple-element.119), channel_id=1, source_target_pairs={{0,16},{16,32},{32,48},{48,64},{64,80},{80,96},{96,112},{112,128},... | collective-permute-start | bytes 786440 | tf_op jit(solution)/shard_map/ppermute | solution.py:15
  53.0 4.6 %collective-permute-done.1 = f32[256,256]{1,0:T(8,128)S(1)} collective-permute-done((f32[256,256]{1,0:T(8,128)S(1)}, f32[256,256]{1,0:T(8,128)S(1)}, u32[]{:S(2)}, u32[]{:S(2)}) %collective-permute-start.1) | collective-permute-done | bytes 262176 | tf_op jit(solution)/shard_map/ppermute | solution.py:15
  59.6 2.4 fusion.6
  62.0 1.3 copy.46
  63.3 1.4 fusion.7
  65.7 47.1 %custom-call.20 = f32[4,128,128]{2,1,0:T(8,128)S(1)} custom-call(f32[4,128,128]{2,1,0:T(8,128)S(1)} %cholesky.122), custom_call_target="Cholesky" | custom-call | tf_op jit(solution)/shard_map/jit(cholesky)/cholesky | solution.py:67
  112.9 39.3 %custom-call.21 = f32[4,1,128,128]{2,3,1,0:T(8,128)S(1)} custom-call(f32[4,1,128,128]{3,2,1,0:T(8,128)S(1)} %select_bitcast_fusion), custom_call_target="InvertDiagBlocksLowerTriangular" | custom-call | tf_op jit(solution)/shard_map/jit(cholesky)/cholesky | solution.py:67
  152.2 1.4 constant_dynamic-update-slice_fusion.1
  153.5 1.6 convolution_subtract_fusion.2
  155.2 46.9 %custom-call.22 = f32[4,128,128]{2,1,0:T(8,128)S(1)} custom-call(f32[4,128,128]{2,1,0:T(8,128)S(1)} %convolution_subtract_fusion.2), custom_call_target="Cholesky" | custom-call | tf_op jit(solution)/shard_map/jit(cholesky)/cholesky | solution.py:67
  203.1 1.4 select_select_fusion
  204.6 5.5 %while.9 = (s32[]{:T(128)}, f32[4,256,256]{2,1,0:T(8,128)S(1)}, s32[2,2]{1,0:T(2,128)S(1)}, f32[2,4,128,128]{3,2,0,1:T(8,128)}, s32[]{:T(128)}) while((s32[]{:T(128)}, f32[4,256,256]{2,1,0:T(8,128)S(1)}, s32[2,2]{1,0:T(2,128)S(1)}, f32[2,4,128,128]{3,2,0,1:T(8,128)}, s32[]{:T(128)}) %tuple.65), condition=%wide.while_cond.8, body=%wide.while_body.8.sunk | while | flops 2 | bytes 525421 | solution.py:47
  205.2 2.1 bitcast_dynamic-update-slice_fusion.2
  208.0 2.1 bitcast_dynamic-update-slice_fusion.2
  210.1 79.4 %custom-call.23 = f32[4,2,128,128]{2,3,1,0:T(8,128)S(1)} custom-call(f32[4,2,128,128]{3,2,1,0:T(8,128)} %bitcast.142), custom_call_target="InvertDiagBlocksLowerTriangular" | custom-call | tf_op jit(solution)/shard_map/vmap(jit(_cho_solve))/triangular_solve | solution.py:47
  289.6 1.9 fusion.12
  291.5 2.1 convolution_subtract_fusion.1
  294.2 1.5 fusion.39
  296.4 1.9 fusion.38
  299.7 3.4 fusion.56
  305.7 91.4 %reduce-scatter.2.cloned.1.call-done = f32[16,128]{1,0:T(8,128)} async-done(((f32[256,128]{1,0:T(8,128)}), f32[16,128]{1,0:T(8,128)}) %reduce-scatter.2.cloned.1.call-update) | async-done | bytes 8208 | tf_op jit(solution)/shard_map/reduce_scatter | solution.py:93
  (68 shorter events, 16.6 us)
Async XLA Ops:
  7.2 1.5 copy-start
  7.2 389.9 %reduce-scatter.2.cloned.1.call-start = ((), (), s32[]{:S(2)}) async-start(), calls=%async_computation.1 | async-start | bytes 139264 | tf_op jit(solution)/shard_map/reduce_scatter | solution.py:93
  24.4 35.2 %collective-permute-start.3 = (f32[256,256]{0,1:T(8,128)}, f32[256,256]{0,1:T(8,128)}, u32[]{:S(2)}, u32[]{:S(2)}) collective-permute-start(f32[256,256]{0,1:T(8,128)} %fusion.35), channel_id=1, source_target_pairs={{1,0},{2,1},{3,2},{4,3},{5,4},{6,5},{7,6},{8,7},{9,8},{10,9},{11,1... | collective-permute-start | bytes 786440 | tf_op jit(solution)/shard_map/ppermute | solution.py:15
  29.2 10.3 %copy-start.4 = (bf16[1,1,4,256,256]{4,3,2,1,0:T(8,128)(2,1)S(1)}, bf16[1,1,4,256,256]{4,3,2,1,0:T(8,128)(2,1)}, u32[]{:S(2)}) copy-start(bf16[1,1,4,256,256]{4,3,2,1,0:T(8,128)(2,1)} %param.24) | copy-start | bytes 1572868
  29.2 30.4 %collective-permute-start.2 = (f32[256,256]{0,1:T(8,128)S(1)}, f32[256,256]{0,1:T(8,128)}, u32[]{:S(2)}, u32[]{:S(2)}) collective-permute-start(f32[256,256]{0,1:T(8,128)S(1)} %multiply_subtract_fusion), channel_id=1, source_target_pairs={{0,1},{1,2},{2,3},{3,4},{4,5},{5,6},{6,7},{7,8},{8,9},{9,10},{10,1... | collective-permute-start | bytes 786440 | tf_op jit(solution)/shard_map/ppermute | solution.py:15
  38.1 14.4 %copy-start.8 = (s32[1,1,4]{2,1,0:T(1,128)S(1)}, s32[1,1,4]{2,1,0:T(1,128)}, u32[]{:S(2)}) copy-start(s32[1,1,4]{2,1,0:T(1,128)} %param.26) | copy-start | bytes 52
  46.6 11.0 %collective-permute-start.1 = (f32[256,256]{1,0:T(8,128)S(1)}, f32[256,256]{1,0:T(8,128)S(1)}, u32[]{:S(2)}, u32[]{:S(2)}) collective-permute-start(f32[256,256]{1,0:T(8,128)S(1)} %get-tuple-element.118), channel_id=1, source_target_pairs={{16,0},{32,16},{48,32},{64,48},{80,64},{96,80},{112,96},{128,112},... | collective-permute-start | bytes 786440 | tf_op jit(solution)/shard_map/ppermute | solution.py:15
  47.9 10.9 %collective-permute-start = (f32[256,256]{1,0:T(8,128)S(1)}, f32[256,256]{1,0:T(8,128)S(1)}, u32[]{:S(2)}, u32[]{:S(2)}) collective-permute-start(f32[256,256]{1,0:T(8,128)S(1)} %get-tuple-element.119), channel_id=1, source_target_pairs={{0,16},{16,32},{32,48},{48,64},{64,80},{80,96},{96,112},{112,128},... | collective-permute-start | bytes 786440 | tf_op jit(solution)/shard_map/ppermute | solution.py:15
  64.7 1.0 copy-start.3
  202.1 1.0 copy-start.2
  289.6 4.0 copy-start.5
  289.6 8.7 %copy-start.6 = (bf16[1,1,256,128]{3,2,1,0:T(8,128)(2,1)S(1)}, bf16[1,1,256,128]{3,2,1,0:T(8,128)(2,1)}, u32[]{:S(2)}) copy-start(bf16[1,1,256,128]{3,2,1,0:T(8,128)(2,1)} %param.25) | copy-start | bytes 196612
  295.8 3.9 copy-start.1
  299.0 4.8 %copy-start.7 = (s32[1,1,128]{2,1,0:T(1,128)S(1)}, s32[1,1,128]{2,1,0:T(1,128)}, u32[]{:S(2)}) copy-start(s32[1,1,128]{2,1,0:T(1,128)} %param.27) | copy-start | bytes 1540
Sparse Core Ops, SparseCore 0:
  304.7 92.3 reduce-scatter.1
where the time goes:
time: 405 us; the launch traced here: 404 us
  other arithmetic  237 us (59%)
  waiting for transfers between devices  96.4 us (24%)
  matrix products  24 us (6%)
  local copies, waits for them, and re-layouts  19.5 us (5%)
  between operations  14.5 us (4%)
  starting transfers between devices  12.4 us (3%)
    another operation x9, other arithmetic, body(): factors = jnp.linalg.cholesky(own_blocks + partners)  134 us
    reduce_scatter x1, waiting for transfers between devices, body(): lax.psum_scatter(jnp.dot(onehot, local, precision=lax.Precision.HIGHEST),...  91.4 us
    another operation x4, other arithmetic, solve_face(): return jax.scipy.linalg.cho_solve((factor_one, True), right_one)  80.9 us
    ppermute x4, starting transfers between devices, shifted(): lax.ppermute(value, axis, [(source, source + steps) for source in range(i...  12.4 us
    another operation x6, matrix products, solve_face(): return jax.scipy.linalg.cho_solve((factor_one, True), right_one)  8.65 us
  transfers between devices with their start and end apart: 5, of which 3 were waited for; matrix products, arithmetic and copies ran while one was open for 5% of the time, Pallas kernels for 0%

commit v1 on v0

v1 whole, which is shorter than its diff:
```python
import functools

import jax
import jax.numpy as jnp
from jax import lax
from jax.experimental import pallas as pl
from jax.experimental.pallas import tpu as pltpu
from jax.sharding import PartitionSpec as P

NI = 768
NF = 256
FACES = 4
MODES = 32
NCG = 256

F32 = jnp.float32
BF16 = jnp.bfloat16
NORTH, SOUTH, WEST, EAST = range(FACES)

SWEEP_TOL = 3e-4
RESIDUAL_TOL = 4e-10
MAX_SQUARINGS = 40
MAX_SWEEPS = 12


def dot(left, right):
    return lax.dot_general(left, right, (((1,), (0,)), ((), ())), preferred_element_type=F32)


def dot_rows(left, right):
    return lax.dot_general(left, right, (((0,), (0,)), ((), ())), preferred_element_type=F32)


def split(value):
    high = value.astype(BF16)
    return high, (value - high.astype(F32)).astype(BF16)


def left_three(value):
    high, low = split(value)
    return jnp.concatenate([high, high, low], axis=1)


def right_three(value):
    high, low = split(value)
    return jnp.concatenate([high, low, high], axis=0)


def odd_column():
    return lax.rem(lax.axis_index("gy"), 2) == 1


def own_kernel(first, by_column, inverse, couple, faces, solved, one, two):
    lower = first * NF
    solved[...] = dot(inverse[...], couple[:, lower : lower + 2 * NF]).astype(BF16)
    blocks = []
    for n in range(2):
        columns = slice(n * NF, (n + 1) * NF)
        gram = dot_rows(couple[:, lower + n * NF : lower + (n + 1) * NF], solved[:, columns])
        blocks.append(faces[first + n].astype(F32) - 0.5 * (gram + gram.T))
    if by_column:
        odd = odd_column()
        one[...] = jnp.where(odd, blocks[1], blocks[0])
        two[...] = jnp.where(odd, blocks[0], blocks[1])
    else:
        one[...], two[...] = blocks


def own_blocks(inverse, couple, faces, first, by_column):
    vmem = pl.BlockSpec(memory_space=pltpu.VMEM)
    block = jax.ShapeDtypeStruct((NF, NF), F32)
    return pl.pallas_call(
        functools.partial(own_kernel, first, by_column),
        out_shape=(jax.ShapeDtypeStruct((NI, 2 * NF), BF16), block, block),
        in_specs=[vmem] * 3,
        out_specs=(vmem,) * 3,
        compiler_params=pltpu.CompilerParams(vmem_limit_bytes=16 << 20),
        cost_estimate=pl.CostEstimate(
            flops=4 * NI * NI * NF + 4 * NI * NF * NF,
            bytes_accessed=2 * NI * NI + 8 * NI * NF + 12 * NF * NF,
            transcendentals=0,
        ),
        name=f"own_blocks_{first}",
    )(inverse, couple, faces)


def eye():
    rows = lax.broadcasted_iota(jnp.int32, (NF, NF), 0)
    columns = lax.broadcasted_iota(jnp.int32, (NF, NF), 1)
    return rows == columns


def coarse_kernel(
    links, sent_north, sent_south, sent_far, sent_near, north, south, far, near,
    modes, couple, solved_ns, solved_we, faces, owners,
    deluxe, partial,
    own, matrix, power, sweep, rest, scale, phi, left, right,
):
    solved = [solved_ns, solved_ns, solved_we, solved_we]
    weight = [links[n].astype(F32) for n in range(FACES)]

    odd = odd_column()
    own[NORTH] = sent_north[...]
    own[SOUTH] = sent_south[...]
    own[WEST] = jnp.where(odd, sent_near[...], sent_far[...])
    own[EAST] = jnp.where(odd, sent_far[...], sent_near[...])

    def partner(n):
        if n in (NORTH, SOUTH):
            return (north, south)[n][...]
        if n == WEST:
            return jnp.where(odd, near[...], far[...])
        return jnp.where(odd, far[...], near[...])

    own_norm = []
    for n in range(FACES):
        m = own[n] + partner(n) * weight[n]
        diagonal = jnp.sum(jnp.where(eye(), m, 0.0), axis=1, keepdims=True)
        inverse_diagonal = 1.0 / diagonal
        bound = jnp.max(jnp.sum(jnp.abs(m), axis=1, keepdims=True) * inverse_diagonal)
        factor = jnp.where(bound < 1.75, 1.0, 1.0 / bound)
        matrix[n] = m
        scale[n] = jnp.broadcast_to(inverse_diagonal * factor, (NF, 128))
        block = own[n]
        rest[n] = block
        deluxe[n] = jnp.zeros((NF, NF), F32)
        own_norm.append(jnp.sum(block * block))

    def scaled(n):
        return jnp.concatenate([scale[n]] * 2, axis=1)

    def largest(values):
        result = values[0]
        for value in values[1:]:
            result = jnp.maximum(result, value)
        return result

    def sweep_once(state):
        count, _, now = state
        norms = []
        for n in range(FACES):
            by = scaled(n)
            first = jnp.where(eye(), 1.0, 0.0) - by * matrix[n]
            start = by * rest[n]
            both = dot(left_three(first), right_three(jnp.concatenate([first, start], axis=1)))
            square = both[:, :NF]
            power[n] = square
            sweep[n] = start + both[:, NF:]
            norms.append(jnp.sum(square * square))

        def more(inner):
            return jnp.logical_and(inner[1] > SWEEP_TOL, inner[0] < MAX_SQUARINGS)

        def squaring(inner):
            found = []
            for n in range(FACES):
                error = power[n]
                start = sweep[n]
                both = dot(left_three(error), right_three(jnp.concatenate([error, start], axis=1)))
                square = both[:, :NF]
                power[n] = square
                sweep[n] = start + both[:, NF:]
                found.append(jnp.sum(square * square))
            return inner[0] + 1, largest(found)

        lax.while_loop(more, squaring, (jnp.int32(0), largest(norms)))

        ratios = []
        for n in range(FACES):
            start = sweep[n]
            total = deluxe[n] + (start + dot(left_three(power[n]), right_three(start)))
            deluxe[n] = total
            residual = own[n] - dot(left_three(matrix[n]), right_three(total))
            rest[n] = residual
            ratios.append(jnp.sum(residual * residual) / own_norm[n])
        return count + 1, now, largest(ratios)

    def unsolved(state):
        count, before, now = state
        return jnp.logical_and(
            jnp.logical_and(now > RESIDUAL_TOL, now < 0.25 * before), count < MAX_SWEEPS
        )

    lax.while_loop(unsolved, sweep_once, (jnp.int32(0), jnp.float32(8.0), jnp.float32(1.0)))

    for n in range(FACES):
        high, low = split(deluxe[n])
        mode = modes[:, n * MODES : (n + 1) * MODES]
        phi[n] = dot(high, mode) + dot(low, mode)

    local = jnp.zeros((FACES * MODES, FACES * MODES), F32)
    rows = lax.broadcasted_iota(jnp.int32, (FACES * MODES, FACES * MODES), 0)
    columns = lax.broadcasted_iota(jnp.int32, (FACES * MODES, FACES * MODES), 1)
    pieces = []
    for n in range(FACES):
        both = jnp.concatenate(split(phi[n]), axis=1)
        lower = n * NF
        one = dot(couple[:, lower : lower + NF], both)
        two = dot(solved[n][:, lower % (2 * NF) : lower % (2 * NF) + NF], both)
        three = dot(faces[n], both)
        here = slice(n * MODES, (n + 1) * MODES)
        left[:, here] = one[:, :MODES] + one[:, MODES:]
        right[:, here] = two[:, :MODES] + two[:, MODES:]
        pieces.append(three[:, :MODES] + three[:, MODES:])
    own_part = dot_three_rows(
        jnp.concatenate([phi[n] for n in range(FACES)], axis=1), jnp.concatenate(pieces, axis=1), True
    )
    cross = dot_three_rows(left[...], right[...], False)
    same = (rows // MODES) == (columns // MODES)
    local = jnp.where(same, own_part, 0.0) - 0.5 * (cross + cross.T)

    def spread(index):
        face = index // MODES
        value = jnp.zeros(index.shape, F32)
        for n in range(FACES):
            value = jnp.where(face == n, weight[n], value)
        return value

    local = local * spread(rows) * spread(columns)
    slots = lax.broadcasted_iota(jnp.int32, (NCG, FACES * MODES), 0)
    onehot = jnp.where(owners[...] == slots, 1.0, 0.0).astype(BF16)
    high, low = split(local)
    lowest = (local - high.astype(F32) - low.astype(F32)).astype(BF16)
    partial[...] = dot(onehot, high) + (dot(onehot, low) + dot(onehot, lowest))


def dot_three_rows(one, two, blocks):
    one_high, one_low = split(one)
    two_high, two_low = split(two)
    return dot_rows(one_high, two_high) + (dot_rows(one_high, two_low) + dot_rows(one_low, two_high))


def coarse_partial(links, sent, received, modes, couple, solved_ns, solved_we, faces, owners):
    vmem = pl.BlockSpec(memory_space=pltpu.VMEM)
    smem = pl.BlockSpec(memory_space=pltpu.SMEM)
    return pl.pallas_call(
        coarse_kernel,
        out_shape=(
            jax.ShapeDtypeStruct((FACES, NF, NF), F32),
            jax.ShapeDtypeStruct((NCG, FACES * MODES), F32),
        ),
        in_specs=[smem] + [vmem] * 14,
        out_specs=(vmem, vmem),
        scratch_shapes=[pltpu.VMEM((FACES, NF, NF), F32)] * 5
        + [
            pltpu.VMEM((FACES, NF, 128), F32),
            pltpu.VMEM((FACES, NF, MODES), F32),
            pltpu.VMEM((NI, FACES * MODES), F32),
            pltpu.VMEM((NI, FACES * MODES), F32),
        ],
        compiler_params=pltpu.CompilerParams(vmem_limit_bytes=28 << 20),
        cost_estimate=pl.CostEstimate(flops=8 << 30, bytes_accessed=4 << 20, transcendentals=0),
        name="coarse_partial",
    )(links, *sent, *received, modes, couple, solved_ns, solved_we, faces, owners)


def swap_pairs(value, axis, first):
    count = lax.axis_size(axis)
    pairs = []
    for low in range(first, count - 1, 2):
        pairs += [(low, low + 1), (low + 1, low)]
    return lax.ppermute(value, axis, pairs)


def shifted(value, axis, steps):
    count = lax.axis_size(axis)
    initial, last = (max(0, -steps), min(count, count - steps))
    return lax.ppermute(value, axis, [(source, source + steps) for source in range(initial, last)])


def body(interior_inverse, coupling, face_matrix, face_modes, face_links, owner_map):
    inverse = interior_inverse[0, 0]
    couple = coupling[0, 0]
    faces = face_matrix[0, 0]
    modes = face_modes[0, 0]
    links = face_links[0, 0]
    owners = owner_map[0]
    solved_we, far, near = own_blocks(inverse, couple, faces, WEST, True)
    far_part = swap_pairs(far, "gy", 1)
    solved_ns, north, south = own_blocks(inverse, couple, faces, NORTH, False)
    north_part = shifted(south, "gx", 1)
    south_part = shifted(north, "gx", -1)
    near_part = swap_pairs(near, "gy", 0)
    deluxe, partial = coarse_partial(
        links, (north, south, far, near), (north_part, south_part, far_part, near_part),
        modes, couple, solved_ns, solved_we, faces, owners,
    )
    count = lax.axis_size("gy")
    parts = partial.reshape(count, NCG // count, FACES * MODES)
    coarse = lax.all_to_all(parts, "gy", 0, 0).sum(0)
    return deluxe[None, None], coarse[None]


def solution(mesh):
    placed = (
        P("gx", "gy", None, None),
        P("gx", "gy", None, None),
        P("gx", "gy", None, None, None),
        P("gx", "gy", None, None),
        P("gx", "gy", None),
        P("gx", "gy", None),
    )
    return jax.shard_map(
        body,
        mesh=mesh,
        in_specs=placed,
        out_specs=(P("gx", "gy", None, None, None), P("gx", "gy", None)),
        check_vma=False,
    )
```

time: 405 us -> 59.4 us (0.15)
  the two profiles are of different devices: /device:TPU:2 before, /device:TPU:9 now
where the time goes in v1:
time: 59.4 us; the launch traced here: 58.9 us
  starting transfers between devices  20.4 us (34%)
  blocking collectives  13.2 us (22%)
  Pallas kernels  11.1 us (19%)
  waiting for transfers between devices  9.14 us (15%)
  local copies, waits for them, and re-layouts  3.75 us (6%)
  between operations  0.76 us (1%)
  other arithmetic  0.62 us (1%)
    ppermute x2, starting transfers between devices, shifted(): lax.ppermute(value, axis, [(source, source + steps) for source in range(i...  13.8 us
    all_to_all x1, blocking collectives, body(): coarse = lax.all_to_all(parts, 'gy', 0, 0).sum(0)  13.2 us
    ppermute x2, waiting for transfers between devices, shifted(): lax.ppermute(value, axis, [(source, source + steps) for source in range(i...  9.14 us
    pallas_call x1, Pallas kernels, coarse_partial(): pl.pallas_call(coarse_kernel, out_shape=(jax.ShapeDtypeStruct((FACES, NF,...  8.87 us
    ppermute x2, starting transfers between devices, swap_pairs(): return lax.ppermute(value, axis, pairs)  6.54 us
    unnamed x16, local copies, waits for them, and re-layouts  3.75 us
    pallas_call x2, Pallas kernels, own_blocks(): pl.pallas_call(functools.partial(own_kernel, first, by_column), out_shape...  2.24 us
  transfers between devices with their start and end apart: 4, of which 2 were waited for; matrix products, arithmetic and copies ran while one was open for 0% of the time, Pallas kernels for 2%

profile of v1, /device:TPU:9, one launch (start us, length us, event | category | flops | bytes accessed | tf_op | source)
XLA Modules:
  0.0 58.9 jit_solution(1978101568922909167)
XLA Ops:
  0.6 0.0 copy-start
  0.6 1.4 %copy-done = bf16[1,1,768,1024]{3,2,1,0:T(8,128)(2,1)S(1)} copy-done((bf16[1,1,768,1024]{3,2,1,0:T(8,128)(2,1)S(1)}, bf16[1,1,768,1024]{3,2,1,0:T(8,128)(2,1)}, u32[]{:S(2)}) %copy-start) | copy-done | bytes 1572888
  2.0 0.0 copy-start.2
  2.0 1.3 %copy-done.2 = bf16[1,1,768,768]{3,2,1,0:T(8,128)(2,1)S(1)} copy-done((bf16[1,1,768,768]{3,2,1,0:T(8,128)(2,1)S(1)}, bf16[1,1,768,768]{3,2,1,0:T(8,128)(2,1)}, u32[]{:S(2)}) %copy-start.2) | copy-done | bytes 1179672
  3.3 0.0 copy-start.3
  3.3 1.0 %copy-done.3 = bf16[1,1,4,256,256]{4,3,2,1,0:T(8,128)(2,1)S(1)} copy-done((bf16[1,1,4,256,256]{4,3,2,1,0:T(8,128)(2,1)S(1)}, bf16[1,1,4,256,256]{4,3,2,1,0:T(8,128)(2,1)}, u32[]{:S(2)}) %copy-start.3) | copy-done | bytes 524312
  4.4 1.1 %own_blocks_2.1 = (bf16[768,512]{1,0:T(8,128)(2,1)S(1)}, f32[256,256]{1,0:T(8,128)S(1)}, f32[256,256]{1,0:T(8,128)S(1)}) custom-call(bf16[768,768]{1,0:T(8,128)(2,1)S(1)} %bitcast.12, bf16[768,1024]{1,0:T(8,128)(2,1)S(1)} %bitcast.9, bf16[4,256,256]{2,1,0:T(8,128)(2,1)S(1)} %bitcast.14), custom_call_target="tpu_custom_call" | custom-call | flops 805306368 | bytes 3538944 | tf_op jit(solution)/shard_map/own_blocks_2/pallas_call | solution.py:72
  5.5 4.5 %collective-permute-start.2 = (f32[256,256]{1,0:T(8,128)S(1)}, f32[256,256]{1,0:T(8,128)S(1)}, u32[]{:S(2)}, u32[]{:S(2)}) collective-permute-start(f32[256,256]{1,0:T(8,128)S(1)} %get-tuple-element.12.sent_far), channel_id=1, source_target_pairs={{1,2},{2,1},{3,4},{4,3},{5,6},{6,5},{7,8},{8,7},{9,10},{10,9},{11,... | collective-permute-start | bytes 786440 | tf_op jit(solution)/shard_map/ppermute | solution.py:262
  10.0 0.0 copy-start.1
  10.0 0.0 copy-start.4
  10.0 0.0 copy-start.5
  10.0 0.0 copy-start.6
  10.0 0.0 copy-start.7
  10.0 2.1 %collective-permute-start.3 = (f32[256,256]{1,0:T(8,128)S(1)}, f32[256,256]{1,0:T(8,128)S(1)}, u32[]{:S(2)}, u32[]{:S(2)}) collective-permute-start(f32[256,256]{1,0:T(8,128)S(1)} %get-tuple-element.13.sent_near), channel_id=1, source_target_pairs={{0,1},{1,0},{2,3},{3,2},{4,5},{5,4},{6,7},{7,6},{8,9},{9,8},{10,11... | collective-permute-start | bytes 786440 | tf_op jit(solution)/shard_map/ppermute | solution.py:262
  12.1 1.1 %own_blocks_0.1 = (bf16[768,512]{1,0:T(8,128)(2,1)S(1)}, f32[256,256]{1,0:T(8,128)S(1)}, f32[256,256]{1,0:T(8,128)S(1)}) custom-call(bf16[768,768]{1,0:T(8,128)(2,1)S(1)} %bitcast.13, bf16[768,1024]{1,0:T(8,128)(2,1)S(1)} %bitcast.10, bf16[4,256,256]{2,1,0:T(8,128)(2,1)S(1)} %bitcast.15), custom_call_target="tpu_custom_call" | custom-call | flops 805306368 | bytes 3538944 | tf_op jit(solution)/shard_map/own_blocks_0/pallas_call | solution.py:72
  13.2 11.9 %collective-permute-start.1 = (f32[256,256]{1,0:T(8,128)S(1)}, f32[256,256]{1,0:T(8,128)S(1)}, u32[]{:S(2)}, u32[]{:S(2)}) collective-permute-start(f32[256,256]{1,0:T(8,128)S(1)} %get-tuple-element.10.sent_north), channel_id=1, source_target_pairs={{16,0},{32,16},{48,32},{64,48},{80,64},{96,80},{112,96},{128,112},... | collective-permute-start | bytes 786440 | tf_op jit(solution)/shard_map/ppermute | solution.py:268
  25.1 1.9 %collective-permute-start = (f32[256,256]{1,0:T(8,128)S(1)}, f32[256,256]{1,0:T(8,128)S(1)}, u32[]{:S(2)}, u32[]{:S(2)}) collective-permute-start(f32[256,256]{1,0:T(8,128)S(1)} %get-tuple-element.11.sent_south), channel_id=1, source_target_pairs={{0,16},{16,32},{32,48},{48,64},{64,80},{80,96},{96,112},{112,128},... | collective-permute-start | bytes 786440 | tf_op jit(solution)/shard_map/ppermute | solution.py:268
  27.1 0.0 collective-permute-done.2.far
  27.1 0.0 collective-permute-done.3.near
  27.1 3.2 %collective-permute-done.1.south = f32[256,256]{1,0:T(8,128)S(1)} collective-permute-done((f32[256,256]{1,0:T(8,128)S(1)}, f32[256,256]{1,0:T(8,128)S(1)}, u32[]{:S(2)}, u32[]{:S(2)}) %collective-permute-start.1) | collective-permute-done | bytes 262176 | tf_op jit(solution)/shard_map/ppermute | solution.py:268
  30.3 5.9 %collective-permute-done.north = f32[256,256]{1,0:T(8,128)S(1)} collective-permute-done((f32[256,256]{1,0:T(8,128)S(1)}, f32[256,256]{1,0:T(8,128)S(1)}, u32[]{:S(2)}, u32[]{:S(2)}) %collective-permute-start) | collective-permute-done | bytes 262176 | tf_op jit(solution)/shard_map/ppermute | solution.py:268
  36.2 0.0 copy-done.1
  36.2 0.0 copy-done.4
  36.2 0.0 copy-done.5
  36.2 0.0 copy-done.6
  36.2 0.0 copy-done.7
  36.3 8.9 %coarse_partial.1 = (f32[4,256,256]{2,1,0:T(8,128)}, f32[256,128]{1,0:T(8,128)S(1)}) custom-call(s32[4]{0:T(128)S(1)} %bitcast.19, f32[256,256]{1,0:T(8,128)S(1)} %get-tuple-element.10.sent_north, f32[256,256]{1,0:T(8,128)S(1)} %get-tuple-element.11.sent_south, f32[256,256]{1,0:T(8,128)S(1)} %get-tuple-element.12.sent_far, ...), custom_call_target="tpu_custom_call" | custom-call | flops 8589934592 | bytes 4194304 | tf_op jit(solution)/shard_map/coarse_partial/pallas_call | solution.py:236
  45.1 13.2 %all_to_all.5 = f32[16,16,128]{2,1,0:T(8,128)S(1)} all-to-all(f32[16,16,128]{2,1,0:T(8,128)S(1)} %bitcast.17), channel_id=1, replica_groups=mesh['gx'=32,'gy'=16] {'gy'}, dimensions={0} | all-to-all | bytes 262144 | tf_op jit(solution)/shard_map/all_to_all | solution.py:290
  58.3 0.6 %reduce_sum.9 = f32[16,128]{1,0:T(8,128)} reduce(f32[16,16,128]{2,1,0:T(8,128)S(1)} %all_to_all.5, f32[]{:T(128)} %constant.0.clone.1), dimensions={0}, to_apply=%region_0.0 | reduce | flops 30720 | bytes 139268 | tf_op jit(solution)/shard_map/reduce_sum | solution.py:290
Async XLA Ops:
  0.6 1.4 %copy-start = (bf16[1,1,768,1024]{3,2,1,0:T(8,128)(2,1)S(1)}, bf16[1,1,768,1024]{3,2,1,0:T(8,128)(2,1)}, u32[]{:S(2)}) copy-start(bf16[1,1,768,1024]{3,2,1,0:T(8,128)(2,1)} %param.7) | copy-start | bytes 4718596
  2.0 1.3 %copy-start.2 = (bf16[1,1,768,768]{3,2,1,0:T(8,128)(2,1)S(1)}, bf16[1,1,768,768]{3,2,1,0:T(8,128)(2,1)}, u32[]{:S(2)}) copy-start(bf16[1,1,768,768]{3,2,1,0:T(8,128)(2,1)} %param.6) | copy-start | bytes 3538948
  3.3 1.0 %copy-start.3 = (bf16[1,1,4,256,256]{4,3,2,1,0:T(8,128)(2,1)S(1)}, bf16[1,1,4,256,256]{4,3,2,1,0:T(8,128)(2,1)}, u32[]{:S(2)}) copy-start(bf16[1,1,4,256,256]{4,3,2,1,0:T(8,128)(2,1)} %param.8) | copy-start | bytes 1572868
  5.5 21.6 %collective-permute-start.2 = (f32[256,256]{1,0:T(8,128)S(1)}, f32[256,256]{1,0:T(8,128)S(1)}, u32[]{:S(2)}, u32[]{:S(2)}) collective-permute-start(f32[256,256]{1,0:T(8,128)S(1)} %get-tuple-element.12.sent_far), channel_id=1, source_target_pairs={{1,2},{2,1},{3,4},{4,3},{5,6},{6,5},{7,8},{8,7},{9,10},{10,9},{11,... | collective-permute-start | bytes 786440 | tf_op jit(solution)/shard_map/ppermute | solution.py:262
  10.0 26.2 %copy-start.1 = (bf16[1,1,768,1024]{3,2,1,0:T(8,128)(2,1)S(1)}, bf16[1,1,768,1024]{3,2,1,0:T(8,128)(2,1)}, u32[]{:S(2)}) copy-start(bf16[1,1,768,1024]{3,2,1,0:T(8,128)(2,1)} %param.7) | copy-start | bytes 4718596
  10.0 26.2 %copy-start.4 = (bf16[1,1,4,256,256]{4,3,2,1,0:T(8,128)(2,1)S(1)}, bf16[1,1,4,256,256]{4,3,2,1,0:T(8,128)(2,1)}, u32[]{:S(2)}) copy-start(bf16[1,1,4,256,256]{4,3,2,1,0:T(8,128)(2,1)} %param.8) | copy-start | bytes 1572868
  10.0 26.2 %copy-start.5 = (bf16[1,1,256,128]{3,2,1,0:T(8,128)(2,1)S(1)}, bf16[1,1,256,128]{3,2,1,0:T(8,128)(2,1)}, u32[]{:S(2)}) copy-start(bf16[1,1,256,128]{3,2,1,0:T(8,128)(2,1)} %param.9) | copy-start | bytes 196612
  10.0 26.2 %copy-start.6 = (s32[1,1,4]{2,1,0:T(1,128)S(1)}, s32[1,1,4]{2,1,0:T(1,128)}, u32[]{:S(2)}) copy-start(s32[1,1,4]{2,1,0:T(1,128)} %param.10) | copy-start | bytes 52
  10.0 26.2 %copy-start.7 = (s32[1,1,128]{2,1,0:T(1,128)S(1)}, s32[1,1,128]{2,1,0:T(1,128)}, u32[]{:S(2)}) copy-start(s32[1,1,128]{2,1,0:T(1,128)} %param.11) | copy-start | bytes 1540
  10.0 17.0 %collective-permute-start.3 = (f32[256,256]{1,0:T(8,128)S(1)}, f32[256,256]{1,0:T(8,128)S(1)}, u32[]{:S(2)}, u32[]{:S(2)}) collective-permute-start(f32[256,256]{1,0:T(8,128)S(1)} %get-tuple-element.13.sent_near), channel_id=1, source_target_pairs={{0,1},{1,0},{2,3},{3,2},{4,5},{5,4},{6,7},{7,6},{8,9},{9,8},{10,11... | collective-permute-start | bytes 786440 | tf_op jit(solution)/shard_map/ppermute | solution.py:262
  13.2 17.1 %collective-permute-start.1 = (f32[256,256]{1,0:T(8,128)S(1)}, f32[256,256]{1,0:T(8,128)S(1)}, u32[]{:S(2)}, u32[]{:S(2)}) collective-permute-start(f32[256,256]{1,0:T(8,128)S(1)} %get-tuple-element.10.sent_north), channel_id=1, source_target_pairs={{16,0},{32,16},{48,32},{64,48},{80,64},{96,80},{112,96},{128,112},... | collective-permute-start | bytes 786440 | tf_op jit(solution)/shard_map/ppermute | solution.py:268
  25.1 11.1 %collective-permute-start = (f32[256,256]{1,0:T(8,128)S(1)}, f32[256,256]{1,0:T(8,128)S(1)}, u32[]{:S(2)}, u32[]{:S(2)}) collective-permute-start(f32[256,256]{1,0:T(8,128)S(1)} %get-tuple-element.11.sent_south), channel_id=1, source_target_pairs={{0,16},{16,32},{32,48},{48,64},{64,80},{80,96},{96,112},{112,128},... | collective-permute-start | bytes 786440 | tf_op jit(solution)/shard_map/ppermute | solution.py:268

commit v2 on v1

v2 whole, which is shorter than its diff:
```python
import functools

import jax
import jax.numpy as jnp
from jax import lax
from jax.experimental import pallas as pl
from jax.experimental.pallas import tpu as pltpu
from jax.sharding import PartitionSpec as P

NI = 768
NF = 256
FACES = 4
MODES = 32
NCG = 256
HALF = NF // 2

F32 = jnp.float32
BF16 = jnp.bfloat16
NORTH, SOUTH, WEST, EAST = range(FACES)

SWEEP_TOL = 3e-4
RESIDUAL_TOL = 4e-10
BOUND = 2e-5
MAX_SQUARINGS = 40
MAX_SWEEPS = 12


def dot(left, right):
    return lax.dot_general(left, right, (((1,), (0,)), ((), ())), preferred_element_type=F32)


def dot_rows(left, right):
    return lax.dot_general(left, right, (((0,), (0,)), ((), ())), preferred_element_type=F32)


def split(value):
    high = value.astype(BF16)
    return high, (value - high.astype(F32)).astype(BF16)


def left_three(value):
    high, low = split(value)
    return jnp.concatenate([high, high, low], axis=1)


def right_three(value):
    high, low = split(value)
    return jnp.concatenate([high, low, high], axis=0)


def odd_column():
    return lax.rem(lax.axis_index("gy"), 2) == 1


def grid_iota(rows, columns, dimension):
    return lax.broadcasted_iota(jnp.int32, (rows, columns), dimension)


def pack(block):
    first, last = block[:HALF, :HALF], block[HALF:, HALF:]
    rows, columns = grid_iota(HALF, HALF, 0), grid_iota(HALF, HALF, 1)
    diagonal = jnp.sum(jnp.where(rows == columns, last, 0.0), axis=0, keepdims=True)
    square = jnp.where(rows >= columns, first, last)
    return square, block[:HALF, HALF:], jnp.broadcast_to(diagonal, (8, HALF))


def unpack(packed):
    square, corner, diagonal = packed[:HALF], packed[HALF:NF], packed[NF : NF + 1]
    rows, columns = grid_iota(HALF, HALF, 0), grid_iota(HALF, HALF, 1)
    turned = square.T
    first = jnp.where(rows >= columns, square, turned)
    last = jnp.where(rows == columns, diagonal, jnp.where(rows < columns, square, turned))
    return first, corner, corner.T, last


def own_kernel(
    inverse_hbm, couple_hbm, faces_hbm,
    solved, own, send_north, send_south, send_far, send_near,
    inverse, couple, faces, sems,
):
    third, half = NI // 3, 2 * NF
    copies = [
        pltpu.make_async_copy(couple_hbm.at[:, half:], couple.at[:, half:], sems.at[0]),
        *(
            pltpu.make_async_copy(
                inverse_hbm.at[pl.ds(n * third, third)], inverse.at[pl.ds(n * third, third)], sems.at[1 + n]
            )
            for n in range(3)
        ),
        pltpu.make_async_copy(faces_hbm, faces, sems.at[4]),
        pltpu.make_async_copy(couple_hbm.at[:, :half], couple.at[:, :half], sems.at[5]),
    ]
    for copy in copies:
        copy.start()
    copies[0].wait()
    for n in range(3):
        copies[1 + n].wait()
        rows = slice(n * third, (n + 1) * third)
        solved[rows, half:] = dot(inverse[rows, :], couple[:, half:]).astype(BF16)
    copies[4].wait()

    def own_of(n):
        columns = slice(n * NF, (n + 1) * NF)
        gram = dot_rows(couple[:, columns], solved[:, columns])
        block = faces[n].astype(F32) - 0.5 * (gram + gram.T)
        own[n] = block
        return pack(block)

    def put(ref, parts):
        ref[:HALF], ref[HALF:NF], ref[NF:] = parts

    odd = odd_column()
    west, east = own_of(WEST), own_of(EAST)
    put(send_far, [jnp.where(odd, e, w) for w, e in zip(west, east, strict=True)])
    put(send_near, [jnp.where(odd, w, e) for w, e in zip(west, east, strict=True)])
    copies[5].wait()
    solved[:, :half] = dot(inverse[...], couple[:, :half]).astype(BF16)
    put(send_north, own_of(NORTH))
    put(send_south, own_of(SOUTH))


def own_blocks(inverse, couple, faces):
    vmem = pl.BlockSpec(memory_space=pltpu.VMEM)
    hbm = pl.BlockSpec(memory_space=pltpu.HBM)
    send = jax.ShapeDtypeStruct((NF + 8, HALF), F32)
    return pl.pallas_call(
        own_kernel,
        out_shape=(
            jax.ShapeDtypeStruct((NI, FACES * NF), BF16),
            jax.ShapeDtypeStruct((FACES, NF, NF), F32),
            send, send, send, send,
        ),
        in_specs=[hbm] * 3,
        out_specs=(vmem,) * 6,
        scratch_shapes=[
            pltpu.VMEM((NI, NI), BF16),
            pltpu.VMEM((NI, FACES * NF), BF16),
            pltpu.VMEM((FACES, NF, NF), BF16),
            pltpu.SemaphoreType.DMA((6,)),
        ],
        compiler_params=pltpu.CompilerParams(vmem_limit_bytes=20 << 20),
        name="own_blocks",
    )(*(pltpu.with_memory_space_constraint(value, pltpu.HBM) for value in (inverse, couple, faces)))


def eye():
    rows = lax.broadcasted_iota(jnp.int32, (NF, NF), 0)
    columns = lax.broadcasted_iota(jnp.int32, (NF, NF), 1)
    return rows == columns


def largest(values):
    result = values[0]
    for value in values[1:]:
        result = jnp.maximum(result, value)
    return result


def total_square(value):
    rows = jnp.sum(value * value, axis=0, keepdims=True)
    return jnp.sum(rows, axis=1, keepdims=True)


def general_solve(own, deluxe, matrix, scale, sweep, rest, power):
    own_norm = []
    for n in range(FACES):
        m, block = matrix[n], own[n]
        by = 1.0 / jnp.sum(jnp.where(eye(), m, 0.0), axis=1, keepdims=True)
        bound = jnp.max(jnp.sum(jnp.abs(m), axis=1, keepdims=True) * by)
        factor = jnp.where(bound < 1.75, 1.0, 1.0 / bound)
        scale[n] = jnp.broadcast_to(by * factor, (NF, HALF))
        rest[n] = block
        deluxe[n] = jnp.zeros((NF, NF), F32)
        own_norm.append(jnp.sum(block * block))

    def sweep_once(state):
        count, _, now = state
        for n in range(FACES):
            by = jnp.concatenate([scale[n]] * 2, axis=1)
            power[n] = jnp.where(eye(), 1.0, 0.0) - by * matrix[n]
            sweep[n] = by * rest[n]

        def more(inner):
            return jnp.logical_and(inner[1] > SWEEP_TOL, inner[0] < MAX_SQUARINGS)

        def squaring(inner):
            found = []
            for n in range(FACES):
                error = power[n]
                start = sweep[n]
                both = dot(left_three(error), right_three(jnp.concatenate([error, start], axis=1)))
                square = both[:, :NF]
                power[n] = square
                sweep[n] = start + both[:, NF:]
                found.append(jnp.sum(square * square))
            return inner[0] + 1, largest(found)

        lax.while_loop(more, squaring, (jnp.int32(0), jnp.float32(1.0)))

        ratios = []
        for n in range(FACES):
            start = sweep[n]
            total = deluxe[n] + (start + dot(left_three(power[n]), right_three(start)))
            deluxe[n] = total
            residual = own[n] - dot(left_three(matrix[n]), right_three(total))
            rest[n] = residual
            ratios.append(jnp.sum(residual * residual) / own_norm[n])
        return count + 1, now, largest(ratios)

    def unsolved(state):
        count, before, now = state
        return jnp.logical_and(
            jnp.logical_and(now > RESIDUAL_TOL, now < 0.25 * before), count < MAX_SWEEPS
        )

    lax.while_loop(unsolved, sweep_once, (jnp.int32(0), jnp.float32(8.0), jnp.float32(1.0)))


def coarse_kernel(
    links, own, north, south, far, near, modes, couple, solved, faces, owners,
    deluxe, partial,
    matrix, scale, power, sweep, rest, phi, left, right,
):
    weight = [links[n].astype(F32) for n in range(FACES)]
    odd = odd_column()
    packed = [
        north[...],
        south[...],
        jnp.where(odd, near[...], far[...]),
        jnp.where(odd, far[...], near[...]),
    ]
    for n in range(FACES):
        quarters = unpack(packed[n])
        for at, quarter in enumerate(quarters):
            here = (slice((at // 2) * HALF, (at // 2 + 1) * HALF), slice((at % 2) * HALF, (at % 2 + 1) * HALF))
            matrix[(n, *here)] = own[(n, *here)] + quarter * weight[n]

    def inverse_diagonal(n):
        return 1.0 / jnp.sum(jnp.where(eye(), matrix[n], 0.0), axis=1, keepdims=True)

    norms = [[] for _ in range(FACES)]
    for n in range(FACES):
        by = inverse_diagonal(n)
        scale[n] = jnp.broadcast_to(by, (NF, HALF))
        first = jnp.where(eye(), 0.0, -by * matrix[n])
        norms[n].append(total_square(first))
        start = by * own[n]
        power[0, n] = first.astype(BF16)
        both = dot(power[0, n], jnp.concatenate([power[0, n], start.astype(BF16)], axis=1))
        square = both[:, :NF]
        norms[n].append(total_square(square))
        power[1, n] = square.astype(BF16)
        sweep[n] = start + both[:, NF:]
    for n in range(FACES):
        start = sweep[n]
        rounded = (start + dot(power[1, n], start.astype(BF16))).astype(BF16)
        high, low = split(matrix[n])
        residual = own[n] - (dot(high, rounded) + dot(low, rounded))
        rest[n] = jnp.concatenate([scale[n]] * 2, axis=1) * residual
        rounded = rounded.astype(F32)
        norms[n].append(total_square(rounded))
        deluxe[n] = rounded
    for n in range(FACES):
        start = rest[n]
        sweep[n] = start + dot(power[0, n], start.astype(BF16))
    left_out = []
    for n in range(FACES):
        start = sweep[n]
        step = start + dot(power[1, n], start.astype(BF16))
        deluxe[n] = deluxe[n] + step
        first, square, size = (jnp.sqrt(norm) for norm in norms[n])
        rate = norms[n][1] + (first + square) * (1.0 + first) * 2.0**-8
        left_out.append(rate * jnp.sqrt(total_square(step)) / size)
    worst = largest(left_out)

    @pl.when(jnp.logical_not(jnp.max(worst) < BOUND))
    def _():
        general_solve(own, deluxe, matrix, scale, sweep, rest, phi)

    for n in range(FACES):
        high, low = split(deluxe[n])
        mode = modes[:, n * MODES : (n + 1) * MODES]
        phi[n, :, :MODES] = dot(high, mode) + dot(low, mode)

    local = jnp.zeros((FACES * MODES, FACES * MODES), F32)
    rows = lax.broadcasted_iota(jnp.int32, (FACES * MODES, FACES * MODES), 0)
    columns = lax.broadcasted_iota(jnp.int32, (FACES * MODES, FACES * MODES), 1)
    pieces = []
    for n in range(FACES):
        both = jnp.concatenate(split(phi[n, :, :MODES]), axis=1)
        lower = n * NF
        one = dot(couple[:, lower : lower + NF], both)
        two = dot(solved[:, lower : lower + NF], both)
        three = dot(faces[n], both)
        here = slice(n * MODES, (n + 1) * MODES)
        left[:, here] = one[:, :MODES] + one[:, MODES:]
        right[:, here] = two[:, :MODES] + two[:, MODES:]
        pieces.append(three[:, :MODES] + three[:, MODES:])
    own_part = dot_three_rows(
        jnp.concatenate([phi[n, :, :MODES] for n in range(FACES)], axis=1), jnp.concatenate(pieces, axis=1), True
    )
    cross = dot_three_rows(left[...], right[...], False)
    same = (rows // MODES) == (columns // MODES)
    local = jnp.where(same, own_part, 0.0) - 0.5 * (cross + cross.T)

    def spread(index):
        face = index // MODES
        value = jnp.zeros(index.shape, F32)
        for n in range(FACES):
            value = jnp.where(face == n, weight[n], value)
        return value

    local = local * spread(rows) * spread(columns)
    slots = lax.broadcasted_iota(jnp.int32, (NCG, FACES * MODES), 0)
    onehot = jnp.where(owners[...] == slots, 1.0, 0.0).astype(BF16)
    high, low = split(local)
    lowest = (local - high.astype(F32) - low.astype(F32)).astype(BF16)
    partial[...] = dot(onehot, high) + (dot(onehot, low) + dot(onehot, lowest))


def dot_three_rows(one, two, blocks):
    one_high, one_low = split(one)
    two_high, two_low = split(two)
    return dot_rows(one_high, two_high) + (dot_rows(one_high, two_low) + dot_rows(one_low, two_high))


def coarse_partial(links, own, received, modes, couple, solved, faces, owners):
    vmem = pl.BlockSpec(memory_space=pltpu.VMEM)
    smem = pl.BlockSpec(memory_space=pltpu.SMEM)
    return pl.pallas_call(
        coarse_kernel,
        out_shape=(
            jax.ShapeDtypeStruct((FACES, NF, NF), F32),
            jax.ShapeDtypeStruct((NCG, FACES * MODES), F32),
        ),
        in_specs=[smem] + [vmem] * 10,
        out_specs=(vmem, vmem),
        scratch_shapes=[
            pltpu.VMEM((FACES, NF, NF), F32),
            pltpu.VMEM((FACES, NF, HALF), F32),
            pltpu.VMEM((2, FACES, NF, NF), BF16),
            pltpu.VMEM((FACES, NF, NF), F32),
            pltpu.VMEM((FACES, NF, NF), F32),
            pltpu.VMEM((FACES, NF, NF), F32),
            pltpu.VMEM((NI, FACES * MODES), F32),
            pltpu.VMEM((NI, FACES * MODES), F32),
        ],
        compiler_params=pltpu.CompilerParams(vmem_limit_bytes=32 << 20),
        cost_estimate=pl.CostEstimate(flops=4 << 30, bytes_accessed=4 << 20, transcendentals=0),
        name="coarse_partial",
    )(links, own, *received, modes, couple, solved, faces, owners)


def swap_pairs(value, axis, first):
    count = lax.axis_size(axis)
    pairs = []
    for low in range(first, count - 1, 2):
        pairs += [(low, low + 1), (low + 1, low)]
    return lax.ppermute(value, axis, pairs)


def shifted(value, axis, steps):
    count = lax.axis_size(axis)
    initial, last = (max(0, -steps), min(count, count - steps))
    return lax.ppermute(value, axis, [(source, source + steps) for source in range(initial, last)])


def body(interior_inverse, coupling, face_matrix, face_modes, face_links, owner_map):
    inverse = interior_inverse[0, 0]
    couple = coupling[0, 0]
    faces = face_matrix[0, 0]
    modes = face_modes[0, 0]
    links = face_links[0, 0]
    owners = owner_map[0]
    solved, own, north, south, far, near = own_blocks(inverse, couple, faces)
    far_part = swap_pairs(far, "gy", 1)
    north_part = shifted(south, "gx", 1)
    south_part = shifted(north, "gx", -1)
    near_part = swap_pairs(near, "gy", 0)
    received = (north_part, south_part, far_part, near_part)
    deluxe, partial = coarse_partial(links, own, received, modes, couple, solved, faces, owners)
    count = lax.axis_size("gy")
    parts = partial.reshape(count, NCG // count, FACES * MODES)
    coarse = lax.all_to_all(parts, "gy", 0, 0).sum(0)
    return deluxe[None, None], coarse[None]


def solution(mesh):
    placed = (
        P("gx", "gy", None, None),
        P("gx", "gy", None, None),
        P("gx", "gy", None, None, None),
        P("gx", "gy", None, None),
        P("gx", "gy", None),
        P("gx", "gy", None),
    )
    return jax.shard_map(
        body,
        mesh=mesh,
        in_specs=placed,
        out_specs=(P("gx", "gy", None, None, None), P("gx", "gy", None)),
        check_vma=False,
    )
```

time: 59.4 us -> 49.3 us (0.83)
  waiting for transfers between devices: 9.14 us -> 1.44 us
  local copies, waits for them, and re-layouts: 3.75 us -> 0.02 us
  blocking collectives: 13.2 us -> 15.6 us
    ppermute x2, waiting for transfers between devices: 9.14 us -> 0.01 us  [shifted(): lax.ppermute(value, axis, [(source, source + steps) for source in range(i...]
    unnamed x16 -> x10, local copies, waits for them, and re-layouts: 3.75 us -> 0.02 us
    all_to_all x1, blocking collectives: 13.2 us -> 15.6 us  [body(): coarse = lax.all_to_all(parts, 'gy', 0, 0).sum(0)]
    pallas_call x1, Pallas kernels: 8.87 us -> 6.53 us  [coarse_partial(): pl.pallas_call(coarse_kernel, out_shape=(jax.ShapeDtypeStruct((FACES, NF,...]
    pallas_call x2 -> x1, Pallas kernels: 2.24 us -> 4.25 us  [own_blocks(): pl.pallas_call(own_kernel, out_shape=(jax.ShapeDtypeStruct((NI, FACES * N...]
    ppermute x2, waiting for transfers between devices: 0.01 us -> 1.44 us  [swap_pairs(): return lax.ppermute(value, axis, pairs)]
    ppermute x2, starting transfers between devices: 13.8 us -> 12.9 us  [shifted(): lax.ppermute(value, axis, [(source, source + steps) for source in range(i...]
  transfers between devices with their start and end apart: 4 -> 4, of which waited for: 2 -> 1; matrix products, arithmetic and copies ran while one was open for 0% -> 0% of each run, Pallas kernels for 2% -> 0%
where the time goes in v2:
time: 49.3 us; the launch traced here: 49.1 us
  starting transfers between devices  19.9 us (40%)
  blocking collectives  15.6 us (32%)
  Pallas kernels  10.8 us (22%)
  waiting for transfers between devices  1.44 us (3%)
  between operations  0.75 us (2%)
  other arithmetic  0.62 us (1%)
    all_to_all x1, blocking collectives, body(): coarse = lax.all_to_all(parts, 'gy', 0, 0).sum(0)  15.6 us
    ppermute x2, starting transfers between devices, shifted(): lax.ppermute(value, axis, [(source, source + steps) for source in range(i...  12.9 us
    ppermute x2, starting transfers between devices, swap_pairs(): return lax.ppermute(value, axis, pairs)  6.98 us
    pallas_call x1, Pallas kernels, coarse_partial(): pl.pallas_call(coarse_kernel, out_shape=(jax.ShapeDtypeStruct((FACES, NF,...  6.53 us
    pallas_call x1, Pallas kernels, own_blocks(): pl.pallas_call(own_kernel, out_shape=(jax.ShapeDtypeStruct((NI, FACES * N...  4.25 us
    ppermute x2, waiting for transfers between devices, swap_pairs(): return lax.ppermute(value, axis, pairs)  1.44 us
  transfers between devices with their start and end apart: 4, of which 1 were waited for; matrix products, arithmetic and copies ran while one was open for 0% of the time, Pallas kernels for 0%

profile of v2, /device:TPU:9, one launch (start us, length us, event | category | flops | bytes accessed | tf_op | source)
XLA Modules:
  0.0 49.1 jit_solution(18055781141282827707)
XLA Ops:
  0.6 0.0 copy-start
  0.6 0.0 copy-start.1
  0.7 0.0 copy-start.2
  0.7 0.0 copy-start.3
  0.7 0.0 copy-start.4
  0.7 4.3 %own_blocks.1 = (bf16[768,1024]{1,0:T(8,128)(2,1)S(1)}, f32[4,256,256]{2,1,0:T(8,128)S(1)}, f32[264,128]{1,0:T(8,128)S(1)}, f32[264,128]{1,0:T(8,128)S(1)}, f32[...) custom-call(bf16[768,768]{1,0:T(8,128)(2,1)} %bitcast.17, bf16[768,1024]{1,0:T(8,128)(2,1)} %bitcast.9, ...), custom_call_target="tpu_custom_call" | custom-call | tf_op jit(solution)/shard_map/own_blocks/pallas_call | solution.py:126
  4.9 3.5 %collective-permute-start = (f32[264,128]{1,0:T(8,128)S(1)}, f32[264,128]{1,0:T(8,128)S(1)}, u32[]{:S(2)}, u32[]{:S(2)}) collective-permute-start(f32[264,128]{1,0:T(8,128)S(1)} %get-tuple-element.11), channel_id=1, source_target_pairs={{0,16},{16,32},{32,48},{48,64},{64,80},{80,96},{96,112},{112,128},... | collective-permute-start | bytes 405512 | tf_op jit(solution)/shard_map/ppermute | solution.py:365
  8.5 9.4 %collective-permute-start.1 = (f32[264,128]{1,0:T(8,128)S(1)}, f32[264,128]{1,0:T(8,128)S(1)}, u32[]{:S(2)}, u32[]{:S(2)}) collective-permute-start(f32[264,128]{1,0:T(8,128)S(1)} %get-tuple-element.12), channel_id=1, source_target_pairs={{16,0},{32,16},{48,32},{64,48},{80,64},{96,80},{112,96},{128,112},... | collective-permute-start | bytes 405512 | tf_op jit(solution)/shard_map/ppermute | solution.py:365
  17.9 5.1 %collective-permute-start.2 = (f32[264,128]{1,0:T(8,128)S(1)}, f32[264,128]{1,0:T(8,128)S(1)}, u32[]{:S(2)}, u32[]{:S(2)}) collective-permute-start(f32[264,128]{1,0:T(8,128)S(1)} %get-tuple-element.13), channel_id=1, source_target_pairs={{1,2},{2,1},{3,4},{4,3},{5,6},{6,5},{7,8},{8,7},{9,10},{10,9},{11,... | collective-permute-start | bytes 405512 | tf_op jit(solution)/shard_map/ppermute | solution.py:359
  22.9 1.9 %collective-permute-start.3 = (f32[264,128]{1,0:T(8,128)S(1)}, f32[264,128]{1,0:T(8,128)S(1)}, u32[]{:S(2)}, u32[]{:S(2)}) collective-permute-start(f32[264,128]{1,0:T(8,128)S(1)} %get-tuple-element.14), channel_id=1, source_target_pairs={{0,1},{1,0},{2,3},{3,2},{4,5},{5,4},{6,7},{7,6},{8,9},{9,8},{10,11... | collective-permute-start | bytes 405512 | tf_op jit(solution)/shard_map/ppermute | solution.py:359
  24.9 0.0 collective-permute-done.north
  24.9 0.0 collective-permute-done.1.south
  24.9 1.4 %collective-permute-done.2.far = f32[264,128]{1,0:T(8,128)S(1)} collective-permute-done((f32[264,128]{1,0:T(8,128)S(1)}, f32[264,128]{1,0:T(8,128)S(1)}, u32[]{:S(2)}, u32[]{:S(2)}) %collective-permute-start.2) | collective-permute-done | bytes 135200 | tf_op jit(solution)/shard_map/ppermute | solution.py:359
  26.3 0.0 collective-permute-done.3.near
  26.3 0.0 copy-done
  26.3 0.0 copy-done.1
  26.3 0.0 copy-done.2
  26.3 0.0 copy-done.3
  26.4 0.0 copy-done.4
  26.4 6.5 %coarse_partial.1 = (f32[4,256,256]{2,1,0:T(8,128)}, f32[256,128]{1,0:T(8,128)S(1)}) custom-call(s32[4]{0:T(128)S(1)} %bitcast.15, f32[4,256,256]{2,1,0:T(8,128)S(1)} %get-tuple-element.10.own, f32[264,128]{1,0:T(8,128)S(1)} %collective-permute-done.north, f32[264,128]{1,0:T(8,128)S(1)} %collective-permute-done.1.south, ...), custom_call_target="tpu_custom_call" | custom-call | flops 4294967296 | bytes 4194304 | tf_op jit(solution)/shard_map/coarse_partial/pallas_call | solution.py:330
  32.9 15.6 %all_to_all.5 = f32[16,16,128]{2,1,0:T(8,128)S(1)} all-to-all(f32[16,16,128]{2,1,0:T(8,128)S(1)} %bitcast.13), channel_id=1, replica_groups=mesh['gx'=32,'gy'=16] {'gy'}, dimensions={0} | all-to-all | bytes 262144 | tf_op jit(solution)/shard_map/all_to_all | solution.py:384
  48.4 0.6 %reduce_sum.9 = f32[16,128]{1,0:T(8,128)} reduce(f32[16,16,128]{2,1,0:T(8,128)S(1)} %all_to_all.5, f32[]{:T(128)} %constant.0.clone.1), dimensions={0}, to_apply=%region_0.0 | reduce | flops 30720 | bytes 139268 | tf_op jit(solution)/shard_map/reduce_sum | solution.py:384
Async XLA Ops:
  0.6 25.7 %copy-start = (bf16[1,1,768,1024]{3,2,1,0:T(8,128)(2,1)S(1)}, bf16[1,1,768,1024]{3,2,1,0:T(8,128)(2,1)}, u32[]{:S(2)}) copy-start(bf16[1,1,768,1024]{3,2,1,0:T(8,128)(2,1)} %param.7) | copy-start | bytes 4718596
  0.6 25.7 %copy-start.1 = (bf16[1,1,4,256,256]{4,3,2,1,0:T(8,128)(2,1)S(1)}, bf16[1,1,4,256,256]{4,3,2,1,0:T(8,128)(2,1)}, u32[]{:S(2)}) copy-start(bf16[1,1,4,256,256]{4,3,2,1,0:T(8,128)(2,1)} %param.8) | copy-start | bytes 1572868
  0.7 25.7 %copy-start.2 = (bf16[1,1,256,128]{3,2,1,0:T(8,128)(2,1)S(1)}, bf16[1,1,256,128]{3,2,1,0:T(8,128)(2,1)}, u32[]{:S(2)}) copy-start(bf16[1,1,256,128]{3,2,1,0:T(8,128)(2,1)} %param.9) | copy-start | bytes 196612
  0.7 25.7 %copy-start.3 = (s32[1,1,4]{2,1,0:T(1,128)S(1)}, s32[1,1,4]{2,1,0:T(1,128)}, u32[]{:S(2)}) copy-start(s32[1,1,4]{2,1,0:T(1,128)} %param.10) | copy-start | bytes 52
  0.7 25.7 %copy-start.4 = (s32[1,1,128]{2,1,0:T(1,128)S(1)}, s32[1,1,128]{2,1,0:T(1,128)}, u32[]{:S(2)}) copy-start(s32[1,1,128]{2,1,0:T(1,128)} %param.11) | copy-start | bytes 1540
  4.9 19.9 %collective-permute-start = (f32[264,128]{1,0:T(8,128)S(1)}, f32[264,128]{1,0:T(8,128)S(1)}, u32[]{:S(2)}, u32[]{:S(2)}) collective-permute-start(f32[264,128]{1,0:T(8,128)S(1)} %get-tuple-element.11), channel_id=1, source_target_pairs={{0,16},{16,32},{32,48},{48,64},{64,80},{80,96},{96,112},{112,128},... | collective-permute-start | bytes 405512 | tf_op jit(solution)/shard_map/ppermute | solution.py:365
  8.5 16.4 %collective-permute-start.1 = (f32[264,128]{1,0:T(8,128)S(1)}, f32[264,128]{1,0:T(8,128)S(1)}, u32[]{:S(2)}, u32[]{:S(2)}) collective-permute-start(f32[264,128]{1,0:T(8,128)S(1)} %get-tuple-element.12), channel_id=1, source_target_pairs={{16,0},{32,16},{48,32},{64,48},{80,64},{96,80},{112,96},{128,112},... | collective-permute-start | bytes 405512 | tf_op jit(solution)/shard_map/ppermute | solution.py:365
  17.9 8.4 %collective-permute-start.2 = (f32[264,128]{1,0:T(8,128)S(1)}, f32[264,128]{1,0:T(8,128)S(1)}, u32[]{:S(2)}, u32[]{:S(2)}) collective-permute-start(f32[264,128]{1,0:T(8,128)S(1)} %get-tuple-element.13), channel_id=1, source_target_pairs={{1,2},{2,1},{3,4},{4,3},{5,6},{6,5},{7,8},{8,7},{9,10},{10,9},{11,... | collective-permute-start | bytes 405512 | tf_op jit(solution)/shard_map/ppermute | solution.py:359
  22.9 3.4 %collective-permute-start.3 = (f32[264,128]{1,0:T(8,128)S(1)}, f32[264,128]{1,0:T(8,128)S(1)}, u32[]{:S(2)}, u32[]{:S(2)}) collective-permute-start(f32[264,128]{1,0:T(8,128)S(1)} %get-tuple-element.14), channel_id=1, source_target_pairs={{0,1},{1,0},{2,3},{3,2},{4,5},{5,4},{6,7},{7,6},{8,9},{9,8},{10,11... | collective-permute-start | bytes 405512 | tf_op jit(solution)/shard_map/ppermute | solution.py:359

commit v3 on v2

v3 whole, which is shorter than its diff:
```python
import jax
import jax.numpy as jnp
from jax import lax
from jax.experimental import pallas as pl
from jax.experimental.pallas import tpu as pltpu
from jax.sharding import PartitionSpec as P


NI = 768
NF = 256
FACES = 4
MODES = 32
NCG = 256
HALF = NF // 2

F32 = jnp.float32
BF16 = jnp.bfloat16
NORTH, SOUTH, WEST, EAST = range(FACES)

SWEEP_TOL = 3e-4
RESIDUAL_TOL = 4e-10
BOUND = 2e-5
MAX_SQUARINGS = 40
MAX_SWEEPS = 12


def dot(left, right):
    return lax.dot_general(left, right, (((1,), (0,)), ((), ())), preferred_element_type=F32)


def dot_rows(left, right):
    return lax.dot_general(left, right, (((0,), (0,)), ((), ())), preferred_element_type=F32)


def split(value):
    high = value.astype(BF16)
    return high, (value - high.astype(F32)).astype(BF16)


def left_three(value):
    high, low = split(value)
    return jnp.concatenate([high, high, low], axis=1)


def right_three(value):
    high, low = split(value)
    return jnp.concatenate([high, low, high], axis=0)


def odd_column():
    return lax.rem(lax.axis_index("gy"), 2) == 1


def grid_iota(rows, columns, dimension):
    return lax.broadcasted_iota(jnp.int32, (rows, columns), dimension)


def pack(block):
    first, last = block[:HALF, :HALF], block[HALF:, HALF:]
    rows, columns = grid_iota(HALF, HALF, 0), grid_iota(HALF, HALF, 1)
    diagonal = jnp.sum(jnp.where(rows == columns, last, 0.0), axis=0, keepdims=True)
    square = jnp.where(rows >= columns, first, last)
    return square, block[:HALF, HALF:], jnp.broadcast_to(diagonal, (8, HALF))


def unpack(packed):
    square, corner, diagonal = packed[:HALF], packed[HALF:NF], packed[NF : NF + 1]
    rows, columns = grid_iota(HALF, HALF, 0), grid_iota(HALF, HALF, 1)
    turned = square.T
    first = jnp.where(rows >= columns, square, turned)
    last = jnp.where(rows == columns, diagonal, jnp.where(rows < columns, square, turned))
    return first, corner, corner.T, last


def own_kernel(
    inverse_hbm, couple_hbm, faces_hbm,
    couple, solved, faces, own, send_north, send_south, send_far, send_near,
    inverse, sems,
):
    half = 2 * NF
    third = NI // 3

    def couple_copy(first, at):
        columns = slice(first, first + half)
        return pltpu.make_async_copy(couple_hbm.at[:, columns], couple.at[:, columns], sems.at[at])

    left, right = couple_copy(half, 0), couple_copy(0, 1)
    rows = [slice(n * third, (n + 1) * third) for n in range(3)]
    blocks = [
        pltpu.make_async_copy(inverse_hbm.at[here], inverse.at[here], sems.at[2 + n])
        for n, here in enumerate(rows)
    ]
    faces_copy = pltpu.make_async_copy(faces_hbm, faces, sems.at[5])
    for copy in [left, *blocks, faces_copy, right]:
        copy.start()
    left.wait()
    for block, here in zip(blocks, rows, strict=True):
        block.wait()
        solved[here, half:] = dot(inverse[here, :], couple[:, half:]).astype(BF16)
    faces_copy.wait()

    def own_of(n):
        columns = slice(n * NF, (n + 1) * NF)
        gram = dot_rows(couple[:, columns], solved[:, columns])
        block = faces[n].astype(F32) - 0.5 * (gram + gram.T)
        own[n] = block
        return pack(block)

    def put(ref, parts):
        ref[:HALF], ref[HALF:NF], ref[NF:] = parts

    odd = odd_column()
    pairs = list(zip(own_of(WEST), own_of(EAST), strict=True))
    put(send_far, [jnp.where(odd, e, w) for w, e in pairs])
    put(send_near, [jnp.where(odd, w, e) for w, e in pairs])
    right.wait()
    solved[:, :half] = dot(inverse[...], couple[:, :half]).astype(BF16)
    put(send_north, own_of(NORTH))
    put(send_south, own_of(SOUTH))


def own_blocks(inverse, couple, faces):
    vmem = pl.BlockSpec(memory_space=pltpu.VMEM)
    hbm = pl.BlockSpec(memory_space=pltpu.HBM)
    send = jax.ShapeDtypeStruct((NF + 8, HALF), F32)
    return pl.pallas_call(
        own_kernel,
        out_shape=(
            jax.ShapeDtypeStruct((NI, FACES * NF), BF16),
            jax.ShapeDtypeStruct((NI, FACES * NF), BF16),
            jax.ShapeDtypeStruct((FACES, NF, NF), BF16),
            jax.ShapeDtypeStruct((FACES, NF, NF), F32),
            send, send, send, send,
        ),
        in_specs=[hbm] * 3,
        out_specs=(vmem,) * 8,
        scratch_shapes=[pltpu.VMEM((NI, NI), BF16), pltpu.SemaphoreType.DMA((6,))],
        compiler_params=pltpu.CompilerParams(vmem_limit_bytes=20 << 20),
        name="own_blocks",
    )(*(pltpu.with_memory_space_constraint(value, pltpu.HBM) for value in (inverse, couple, faces)))


def eye():
    rows = lax.broadcasted_iota(jnp.int32, (NF, NF), 0)
    columns = lax.broadcasted_iota(jnp.int32, (NF, NF), 1)
    return rows == columns


def largest(values):
    result = values[0]
    for value in values[1:]:
        result = jnp.maximum(result, value)
    return result


def total_square(value):
    rows = jnp.sum(value * value, axis=0, keepdims=True)
    return jnp.sum(rows, axis=1, keepdims=True)


def general_solve(own, deluxe, matrix, scale, sweep, rest, power):
    own_norm = []
    for n in range(2):
        m, block = matrix[n], own[n]
        by = 1.0 / jnp.sum(jnp.where(eye(), m, 0.0), axis=1, keepdims=True)
        bound = jnp.max(jnp.sum(jnp.abs(m), axis=1, keepdims=True) * by)
        factor = jnp.where(bound < 1.75, 1.0, 1.0 / bound)
        scale[n] = jnp.broadcast_to(by * factor, (NF, HALF))
        rest[n] = block
        deluxe[n] = jnp.zeros((NF, NF), F32)
        own_norm.append(jnp.sum(block * block))

    def sweep_once(state):
        count, _, now = state
        for n in range(2):
            by = jnp.concatenate([scale[n]] * 2, axis=1)
            power[n] = jnp.where(eye(), 1.0, 0.0) - by * matrix[n]
            sweep[n] = by * rest[n]

        def more(inner):
            return jnp.logical_and(inner[1] > SWEEP_TOL, inner[0] < MAX_SQUARINGS)

        def squaring(inner):
            found = []
            for n in range(2):
                error = power[n]
                start = sweep[n]
                both = dot(left_three(error), right_three(jnp.concatenate([error, start], axis=1)))
                square = both[:, :NF]
                power[n] = square
                sweep[n] = start + both[:, NF:]
                found.append(jnp.sum(square * square))
            return inner[0] + 1, largest(found)

        lax.while_loop(more, squaring, (jnp.int32(0), jnp.float32(1.0)))

        ratios = []
        for n in range(2):
            start = sweep[n]
            total = deluxe[n] + (start + dot(left_three(power[n]), right_three(start)))
            deluxe[n] = total
            residual = own[n] - dot(left_three(matrix[n]), right_three(total))
            rest[n] = residual
            ratios.append(jnp.sum(residual * residual) / own_norm[n])
        return count + 1, now, largest(ratios)

    def unsolved(state):
        count, before, now = state
        return jnp.logical_and(
            jnp.logical_and(now > RESIDUAL_TOL, now < 0.25 * before), count < MAX_SWEEPS
        )

    lax.while_loop(unsolved, sweep_once, (jnp.int32(0), jnp.float32(8.0), jnp.float32(1.0)))


def face_weights(links):
    return [links[n].astype(F32) for n in range(FACES)]


def solve_pair(first, weight, own, packed, modes, couple, solved, faces, deluxe, scratch):
    matrix, scale, power, sweep, rest, general, phi = scratch
    own = own.at[first : first + 2]
    for n in range(2):
        quarters = unpack(packed[n])
        for at, quarter in enumerate(quarters):
            here = (slice((at // 2) * HALF, (at // 2 + 1) * HALF), slice((at % 2) * HALF, (at % 2 + 1) * HALF))
            matrix[(n, *here)] = own[(n, *here)] + quarter * weight[first + n]

    norms = [[] for _ in range(2)]
    for n in range(2):
        by = 1.0 / jnp.sum(jnp.where(eye(), matrix[n], 0.0), axis=1, keepdims=True)
        scale[n] = jnp.broadcast_to(by, (NF, HALF))
        factor = jnp.where(eye(), 0.0, -by * matrix[n])
        norms[n].append(total_square(factor))
        start = by * own[n]
        power[0, n] = factor.astype(BF16)
        both = dot(power[0, n], jnp.concatenate([power[0, n], start.astype(BF16)], axis=1))
        square = both[:, :NF]
        norms[n].append(total_square(square))
        power[1, n] = square.astype(BF16)
        sweep[n] = start + both[:, NF:]
    for n in range(2):
        start = sweep[n]
        rounded = (start + dot(power[1, n], start.astype(BF16))).astype(BF16)
        high, low = split(matrix[n])
        residual = own[n] - (dot(high, rounded) + dot(low, rounded))
        rest[n] = jnp.concatenate([scale[n]] * 2, axis=1) * residual
        rounded = rounded.astype(F32)
        norms[n].append(total_square(rounded))
        deluxe[n] = rounded
    for n in range(2):
        start = rest[n]
        sweep[n] = start + dot(power[0, n], start.astype(BF16))
    left_out = []
    for n in range(2):
        start = sweep[n]
        step = start + dot(power[1, n], start.astype(BF16))
        deluxe[n] = deluxe[n] + step
        one, two, size = (jnp.sqrt(norm) for norm in norms[n])
        rate = norms[n][1] + (one + two) * (1.0 + one) * 2.0**-8
        left_out.append(rate * jnp.sqrt(total_square(step)) / size)

    @pl.when(jnp.logical_not(jnp.max(largest(left_out)) < BOUND))
    def _():
        general_solve(own, deluxe, matrix, scale, sweep, rest, general)

    face_of = grid_iota(NF, FACES * MODES, 1) // MODES
    all_phi = jnp.zeros((NF, FACES * MODES), F32)
    for n in range(2):
        mode = jnp.where(face_of == first + n, modes[...].astype(F32), 0.0).astype(BF16)
        mapped = dot(
            jnp.concatenate(split(deluxe[n]), axis=1), jnp.concatenate([mode, mode], axis=0)
        )
        all_phi = all_phi + mapped
        phi[n * NF : (n + 1) * NF, :] = jnp.concatenate(split(mapped), axis=1)

    def times_phi(left):
        both = dot(left, phi[...])
        return both[:, : FACES * MODES] + both[:, FACES * MODES :]

    columns = slice(first * NF, (first + 2) * NF)
    return (
        times_phi(couple[:, columns]),
        times_phi(solved[:, columns]),
        times_phi(jnp.concatenate([faces[first], faces[first + 1]], axis=1)),
        all_phi,
    )


def columns_kernel(
    links, own, far, near, modes, couple, solved, faces,
    deluxe, left, right, faces_phi, all_phi,
    *scratch,
):
    odd = odd_column()
    packed = [jnp.where(odd, near[...], far[...]), jnp.where(odd, far[...], near[...])]
    left[...], right[...], faces_phi[...], all_phi[...] = solve_pair(
        WEST, face_weights(links), own, packed, modes, couple, solved, faces, deluxe, scratch
    )


def rows_kernel(
    links, own, north, south, modes, couple, solved, faces, owners,
    deluxe_we, left_we, right_we, faces_phi_we, all_phi_we,
    deluxe_hbm, partial,
    deluxe, *scratch_sems,
):
    *scratch, sems = scratch_sems
    weight = face_weights(links)
    out_we = pltpu.make_async_copy(deluxe_we, deluxe_hbm.at[WEST:], sems.at[1])
    out_we.start()
    packed = [north[...], south[...]]
    left, right, faces_phi, all_phi = solve_pair(
        NORTH, weight, own, packed, modes, couple, solved, faces, deluxe, scratch
    )
    out = pltpu.make_async_copy(deluxe, deluxe_hbm.at[:WEST], sems.at[0])
    out.start()
    cross = dot_three_rows(left + left_we[...], right + right_we[...])
    own_part = dot_three_rows(all_phi + all_phi_we[...], faces_phi + faces_phi_we[...])
    rows = grid_iota(FACES * MODES, FACES * MODES, 0)
    columns = grid_iota(FACES * MODES, FACES * MODES, 1)
    same = (rows // MODES) == (columns // MODES)
    local = jnp.where(same, own_part, 0.0) - 0.5 * (cross + cross.T)

    def spread(index):
        face = index // MODES
        value = jnp.zeros(index.shape, F32)
        for n in range(FACES):
            value = jnp.where(face == n, weight[n], value)
        return value

    local = local * spread(rows) * spread(columns)
    slots = lax.broadcasted_iota(jnp.int32, (NCG, FACES * MODES), 0)
    onehot = jnp.where(owners[...] == slots, 1.0, 0.0).astype(BF16)
    high, low = split(local)
    lowest = (local - high.astype(F32) - low.astype(F32)).astype(BF16)
    partial[...] = dot(onehot, high) + (dot(onehot, low) + dot(onehot, lowest))
    out_we.wait()
    out.wait()


def dot_three_rows(one, two):
    one_high, one_low = split(one)
    two_high, two_low = split(two)
    return dot_rows(one_high, two_high) + (dot_rows(one_high, two_low) + dot_rows(one_low, two_high))


VMEM_SPEC = pl.BlockSpec(memory_space=pltpu.VMEM)
SMEM_SPEC = pl.BlockSpec(memory_space=pltpu.SMEM)


def pair_scratch():
    square = pltpu.VMEM((2, NF, NF), F32)
    return [
        square,
        pltpu.VMEM((2, NF, HALF), F32),
        pltpu.VMEM((2, 2, NF, NF), BF16),
        square,
        square,
        square,
        pltpu.VMEM((2 * NF, 2 * FACES * MODES), BF16),
    ]


def columns_pair(links, own, far, near, modes, couple, solved, faces):
    tall = jax.ShapeDtypeStruct((NI, FACES * MODES), F32)
    short = jax.ShapeDtypeStruct((NF, FACES * MODES), F32)
    return pl.pallas_call(
        columns_kernel,
        out_shape=(jax.ShapeDtypeStruct((2, NF, NF), F32), tall, tall, short, short),
        in_specs=[SMEM_SPEC] + [VMEM_SPEC] * 7,
        out_specs=(VMEM_SPEC,) * 5,
        scratch_shapes=pair_scratch(),
        compiler_params=pltpu.CompilerParams(vmem_limit_bytes=24 << 20),
        cost_estimate=pl.CostEstimate(flops=2 << 30, bytes_accessed=4 << 20, transcendentals=0),
        name="columns_pair",
    )(links, own, far, near, modes, couple, solved, faces)


def rows_pair(links, own, north, south, modes, couple, solved, faces, owners, of_columns):
    return pl.pallas_call(
        rows_kernel,
        out_shape=(
            jax.ShapeDtypeStruct((FACES, NF, NF), F32),
            jax.ShapeDtypeStruct((NCG, FACES * MODES), F32),
        ),
        in_specs=[SMEM_SPEC] + [VMEM_SPEC] * 13,
        out_specs=(pl.BlockSpec(memory_space=pltpu.HBM), VMEM_SPEC),
        scratch_shapes=[
            pltpu.VMEM((2, NF, NF), F32), *pair_scratch(), pltpu.SemaphoreType.DMA((2,)),
        ],
        compiler_params=pltpu.CompilerParams(vmem_limit_bytes=24 << 20),
        cost_estimate=pl.CostEstimate(flops=3 << 30, bytes_accessed=4 << 20, transcendentals=0),
        name="rows_pair",
    )(links, own, north, south, modes, couple, solved, faces, owners, *of_columns)


def swap_pairs(value, axis, first):
    count = lax.axis_size(axis)
    pairs = []
    for low in range(first, count - 1, 2):
        pairs += [(low, low + 1), (low + 1, low)]
    return lax.ppermute(value, axis, pairs)


def shifted(value, axis, steps):
    count = lax.axis_size(axis)
    initial, last = (max(0, -steps), min(count, count - steps))
    return lax.ppermute(value, axis, [(source, source + steps) for source in range(initial, last)])


def body(interior_inverse, coupling, face_matrix, face_modes, face_links, owner_map):
    inverse = interior_inverse[0, 0]
    couple = coupling[0, 0]
    faces = face_matrix[0, 0]
    modes = face_modes[0, 0]
    links = face_links[0, 0]
    owners = owner_map[0]
    couple, solved, faces, own, north, south, far, near = own_blocks(inverse, couple, faces)
    far_part = swap_pairs(far, "gy", 1)
    near_part = swap_pairs(near, "gy", 0)
    north_part = shifted(south, "gx", 1)
    south_part = shifted(north, "gx", -1)
    of_columns = columns_pair(links, own, far_part, near_part, modes, couple, solved, faces)
    deluxe, partial = rows_pair(
        links, own, north_part, south_part, modes, couple, solved, faces, owners, of_columns
    )
    count = lax.axis_size("gy")
    parts = partial.reshape(count, NCG // count, FACES * MODES)
    coarse = lax.all_to_all(parts, "gy", 0, 0).sum(0)
    return deluxe[None, None], coarse[None]


def solution(mesh):
    placed = (
        P("gx", "gy", None, None),
        P("gx", "gy", None, None),
        P("gx", "gy", None, None, None),
        P("gx", "gy", None, None),
        P("gx", "gy", None),
        P("gx", "gy", None),
    )
    return jax.shard_map(
        body,
        mesh=mesh,
        in_specs=placed,
        out_specs=(P("gx", "gy", None, None, None), P("gx", "gy", None)),
        check_vma=False,
    )
```

time: 49.3 us -> 45.8 us (0.929)
  blocking collectives: 15.6 us -> 12.5 us
  waiting for transfers between devices: 1.44 us -> 0.01 us
  Pallas kernels: 10.8 us -> 11.4 us
    all_to_all x1, blocking collectives: 15.6 us -> 12.5 us  [body(): coarse = lax.all_to_all(parts, 'gy', 0, 0).sum(0)]
    ppermute x2, waiting for transfers between devices: 1.44 us -> 0.01 us  [swap_pairs(): return lax.ppermute(value, axis, pairs)]
    ppermute x2, starting transfers between devices: 12.9 us -> 13.8 us  [shifted(): lax.ppermute(value, axis, [(source, source + steps) for source in range(i...]
    pallas_call x1 -> x2, Pallas kernels: 6.53 us -> 7.24 us  [the longest x1 4.11 us: rows_pair(): pl.pallas_call(rows_kernel, out_shape=(jax.ShapeDtypeStruct((FACES, NF, N...]
    ppermute x2, starting transfers between devices: 6.98 us -> 6.4 us  [swap_pairs(): return lax.ppermute(value, axis, pairs)]
  transfers between devices with their start and end apart: 4 -> 4, of which waited for: 1 -> 0; matrix products, arithmetic and copies ran while one was open for 0% -> 0% of each run, Pallas kernels for 0% -> 7%
where the time goes in v3:
time: 45.8 us; the launch traced here: 45.6 us
  starting transfers between devices  20.2 us (44%)
  blocking collectives  12.5 us (27%)
  Pallas kernels  11.4 us (25%)
  between operations  0.77 us (2%)
  other arithmetic  0.62 us (1%)
    ppermute x2, starting transfers between devices, shifted(): lax.ppermute(value, axis, [(source, source + steps) for source in range(i...  13.8 us
    all_to_all x1, blocking collectives, body(): coarse = lax.all_to_all(parts, 'gy', 0, 0).sum(0)  12.5 us
    ppermute x2, starting transfers between devices, swap_pairs(): return lax.ppermute(value, axis, pairs)  6.4 us
    pallas_call x1, Pallas kernels, own_blocks(): pl.pallas_call(own_kernel, out_shape=(jax.ShapeDtypeStruct((NI, FACES * N...  4.14 us
    pallas_call x1, Pallas kernels, rows_pair(): pl.pallas_call(rows_kernel, out_shape=(jax.ShapeDtypeStruct((FACES, NF, N...  4.11 us
    pallas_call x1, Pallas kernels, columns_pair(): pl.pallas_call(columns_kernel, out_shape=(jax.ShapeDtypeStruct((2, NF, NF...  3.13 us
  transfers between devices with their start and end apart: 4, of which 0 were waited for; matrix products, arithmetic and copies ran while one was open for 0% of the time, Pallas kernels for 7%

profile of v3, /device:TPU:9, one launch (start us, length us, event | category | flops | bytes accessed | tf_op | source)
XLA Modules:
  0.0 45.6 jit_solution(15420167962901070303)
XLA Ops:
  0.6 0.0 copy-start
  0.6 0.0 copy-start.1
  0.7 4.1 %own_blocks.1 = (bf16[768,1024]{1,0:T(8,128)(2,1)S(1)}, bf16[768,1024]{1,0:T(8,128)(2,1)S(1)}, bf16[4,256,256]{2,1,0:T(8,128)(2,1)S(1)}, f32[4,256,256]{2,1,0:T(...) custom-call(bf16[768,768]{1,0:T(8,128)(2,1)} %bitcast.16, ...), custom_call_target="tpu_custom_call" | custom-call | tf_op jit(solution)/shard_map/own_blocks/pallas_call | solution.py:126
  4.8 4.5 %collective-permute-start.2 = (f32[264,128]{1,0:T(8,128)S(1)}, f32[264,128]{1,0:T(8,128)S(1)}, u32[]{:S(2)}, u32[]{:S(2)}) collective-permute-start(f32[264,128]{1,0:T(8,128)S(1)} %get-tuple-element.23), channel_id=1, source_target_pairs={{1,2},{2,1},{3,4},{4,3},{5,6},{6,5},{7,8},{8,7},{9,10},{10,9},{11,... | collective-permute-start | bytes 405512 | tf_op jit(solution)/shard_map/ppermute | solution.py:403
  9.3 1.9 %collective-permute-start.3 = (f32[264,128]{1,0:T(8,128)S(1)}, f32[264,128]{1,0:T(8,128)S(1)}, u32[]{:S(2)}, u32[]{:S(2)}) collective-permute-start(f32[264,128]{1,0:T(8,128)S(1)} %get-tuple-element.24), channel_id=1, source_target_pairs={{0,1},{1,0},{2,3},{3,2},{4,5},{5,4},{6,7},{7,6},{8,9},{9,8},{10,11... | collective-permute-start | bytes 405512 | tf_op jit(solution)/shard_map/ppermute | solution.py:403
  11.2 3.5 %collective-permute-start = (f32[264,128]{1,0:T(8,128)S(1)}, f32[264,128]{1,0:T(8,128)S(1)}, u32[]{:S(2)}, u32[]{:S(2)}) collective-permute-start(f32[264,128]{1,0:T(8,128)S(1)} %get-tuple-element.18), channel_id=1, source_target_pairs={{0,16},{16,32},{32,48},{48,64},{64,80},{80,96},{96,112},{112,128},... | collective-permute-start | bytes 405512 | tf_op jit(solution)/shard_map/ppermute | solution.py:409
  14.8 10.3 %collective-permute-start.1 = (f32[264,128]{1,0:T(8,128)S(1)}, f32[264,128]{1,0:T(8,128)S(1)}, u32[]{:S(2)}, u32[]{:S(2)}) collective-permute-start(f32[264,128]{1,0:T(8,128)S(1)} %get-tuple-element.19), channel_id=1, source_target_pairs={{16,0},{32,16},{48,32},{64,48},{80,64},{96,80},{112,96},{128,112},... | collective-permute-start | bytes 405512 | tf_op jit(solution)/shard_map/ppermute | solution.py:409
  25.1 0.0 collective-permute-done.2.far
  25.1 0.0 collective-permute-done.3.near
  25.1 0.0 copy-done
  25.1 0.0 copy-done.1
  25.1 0.0 copy-start.2
  25.1 3.1 %columns_pair.1 = (f32[2,256,256]{2,1,0:T(8,128)S(1)}, f32[768,128]{1,0:T(8,128)S(1)}, f32[768,128]{1,0:T(8,128)S(1)}, f32[256,128]{1,0:T(8,128)S(1)}, f32[256,128]{1,0:T(8,128)S(1)}) custom-call(s32[4]{0:T(128)S(1)} %bitcast.12, f32[4,256,256]{2,1,0:T(8,128)S(1)} %get-tuple-element.17.own, f32[264,128]{1,0:T(8,128)S(1)} %collective-permute-done.2.far, ...), custom_call_target="tpu_custom_call" | custom-call | flops 2147483648 | bytes 4194304 | tf_op jit(solution)/shard_map/columns_pair/pallas_call | solution.py:368
  28.3 0.0 collective-permute-done.north
  28.3 0.0 collective-permute-done.1.south
  28.3 0.0 copy-done.2
  28.3 4.1 %rows_pair.1 = (f32[4,256,256]{2,1,0:T(8,128)}, f32[256,128]{1,0:T(8,128)S(1)}) custom-call(s32[4]{0:T(128)S(1)} %bitcast.13, f32[4,256,256]{2,1,0:T(8,128)S(1)} %get-tuple-element.17.own, f32[264,128]{1,0:T(8,128)S(1)} %collective-permute-done.north, f32[264,128]{1,0:T(8,128)S(1)} %collective-permute-done.1.south, bf16[256,128]{1,0:T(8,128)(2,1)S(1)} %bitcast.11, ...), custom_call_target="tpu_custom_call" | custom-call | flops 3221225472 | bytes 4194304 | tf_op jit(solution)/shard_map/rows_pair/pallas_call | solution.py:381
  32.4 12.5 %all_to_all.5 = f32[16,16,128]{2,1,0:T(8,128)S(1)} all-to-all(f32[16,16,128]{2,1,0:T(8,128)S(1)} %bitcast.9), channel_id=1, replica_groups=mesh['gx'=32,'gy'=16] {'gy'}, dimensions={0} | all-to-all | bytes 262144 | tf_op jit(solution)/shard_map/all_to_all | solution.py:430
  44.9 0.6 %reduce_sum.9 = f32[16,128]{1,0:T(8,128)} reduce(f32[16,16,128]{2,1,0:T(8,128)S(1)} %all_to_all.5, f32[]{:T(128)} %constant.0.clone.1), dimensions={0}, to_apply=%region_0.0 | reduce | flops 30720 | bytes 139268 | tf_op jit(solution)/shard_map/reduce_sum | solution.py:430
Async XLA Ops:
  0.6 24.5 %copy-start = (bf16[1,1,256,128]{3,2,1,0:T(8,128)(2,1)S(1)}, bf16[1,1,256,128]{3,2,1,0:T(8,128)(2,1)}, u32[]{:S(2)}) copy-start(bf16[1,1,256,128]{3,2,1,0:T(8,128)(2,1)} %param.9) | copy-start | bytes 196612
  0.6 24.5 %copy-start.1 = (s32[1,1,4]{2,1,0:T(1,128)S(1)}, s32[1,1,4]{2,1,0:T(1,128)}, u32[]{:S(2)}) copy-start(s32[1,1,4]{2,1,0:T(1,128)} %param.10) | copy-start | bytes 52
  4.8 20.3 %collective-permute-start.2 = (f32[264,128]{1,0:T(8,128)S(1)}, f32[264,128]{1,0:T(8,128)S(1)}, u32[]{:S(2)}, u32[]{:S(2)}) collective-permute-start(f32[264,128]{1,0:T(8,128)S(1)} %get-tuple-element.23), channel_id=1, source_target_pairs={{1,2},{2,1},{3,4},{4,3},{5,6},{6,5},{7,8},{8,7},{9,10},{10,9},{11,... | collective-permute-start | bytes 405512 | tf_op jit(solution)/shard_map/ppermute | solution.py:403
  9.3 15.8 %collective-permute-start.3 = (f32[264,128]{1,0:T(8,128)S(1)}, f32[264,128]{1,0:T(8,128)S(1)}, u32[]{:S(2)}, u32[]{:S(2)}) collective-permute-start(f32[264,128]{1,0:T(8,128)S(1)} %get-tuple-element.24), channel_id=1, source_target_pairs={{0,1},{1,0},{2,3},{3,2},{4,5},{5,4},{6,7},{7,6},{8,9},{9,8},{10,11... | collective-permute-start | bytes 405512 | tf_op jit(solution)/shard_map/ppermute | solution.py:403
  11.2 17.0 %collective-permute-start = (f32[264,128]{1,0:T(8,128)S(1)}, f32[264,128]{1,0:T(8,128)S(1)}, u32[]{:S(2)}, u32[]{:S(2)}) collective-permute-start(f32[264,128]{1,0:T(8,128)S(1)} %get-tuple-element.18), channel_id=1, source_target_pairs={{0,16},{16,32},{32,48},{48,64},{64,80},{80,96},{96,112},{112,128},... | collective-permute-start | bytes 405512 | tf_op jit(solution)/shard_map/ppermute | solution.py:409
  14.8 13.5 %collective-permute-start.1 = (f32[264,128]{1,0:T(8,128)S(1)}, f32[264,128]{1,0:T(8,128)S(1)}, u32[]{:S(2)}, u32[]{:S(2)}) collective-permute-start(f32[264,128]{1,0:T(8,128)S(1)} %get-tuple-element.19), channel_id=1, source_target_pairs={{16,0},{32,16},{48,32},{64,48},{80,64},{96,80},{112,96},{128,112},... | collective-permute-start | bytes 405512 | tf_op jit(solution)/shard_map/ppermute | solution.py:409
  25.1 3.2 %copy-start.2 = (s32[1,1,128]{2,1,0:T(1,128)S(1)}, s32[1,1,128]{2,1,0:T(1,128)}, u32[]{:S(2)}) copy-start(s32[1,1,128]{2,1,0:T(1,128)} %param.11) | copy-start | bytes 1540

commit v4 on v3

--- a/solution.py
+++ b/solution.py
@@ -47,8 +47,8 @@
     return jnp.concatenate([high, low, high], axis=0)
 
 
-def odd_column():
-    return lax.rem(lax.axis_index("gy"), 2) == 1
+def odd_at(axis):
+    return lax.rem(lax.axis_index(axis), 2) == 1
 
 
 def grid_iota(rows, columns, dimension):
@@ -74,7 +74,7 @@
 
 def own_kernel(
     inverse_hbm, couple_hbm, faces_hbm,
-    couple, solved, faces, own, send_north, send_south, send_far, send_near,
+    couple, solved, faces, own, send_even, send_odd, send_far, send_near,
     inverse, sems,
 ):
     half = 2 * NF
@@ -109,14 +109,15 @@
     def put(ref, parts):
         ref[:HALF], ref[HALF:NF], ref[NF:] = parts
 
-    odd = odd_column()
-    pairs = list(zip(own_of(WEST), own_of(EAST), strict=True))
-    put(send_far, [jnp.where(odd, e, w) for w, e in pairs])
-    put(send_near, [jnp.where(odd, w, e) for w, e in pairs])
+    def put_pair(odd, low, high, up, down):
+        pairs = list(zip(low, high, strict=True))
+        put(up, [jnp.where(odd, l, h) for l, h in pairs])
+        put(down, [jnp.where(odd, h, l) for l, h in pairs])
+
+    put_pair(odd_at("gy"), own_of(WEST), own_of(EAST), send_near, send_far)
     right.wait()
     solved[:, :half] = dot(inverse[...], couple[:, :half]).astype(BF16)
-    put(send_north, own_of(NORTH))
-    put(send_south, own_of(SOUTH))
+    put_pair(odd_at("gx"), own_of(NORTH), own_of(SOUTH), send_even, send_odd)
 
 
 def own_blocks(inverse, couple, faces):
@@ -292,7 +293,7 @@
     deluxe, left, right, faces_phi, all_phi,
     *scratch,
 ):
-    odd = odd_column()
+    odd = odd_at("gy")
     packed = [jnp.where(odd, near[...], far[...]), jnp.where(odd, far[...], near[...])]
     left[...], right[...], faces_phi[...], all_phi[...] = solve_pair(
         WEST, face_weights(links), own, packed, modes, couple, solved, faces, deluxe, scratch
@@ -300,7 +301,7 @@
 
 
 def rows_kernel(
-    links, own, north, south, modes, couple, solved, faces, owners,
+    links, own, even, other, modes, couple, solved, faces, owners,
     deluxe_we, left_we, right_we, faces_phi_we, all_phi_we,
     deluxe_hbm, partial,
     deluxe, *scratch_sems,
@@ -309,7 +310,8 @@
     weight = face_weights(links)
     out_we = pltpu.make_async_copy(deluxe_we, deluxe_hbm.at[WEST:], sems.at[1])
     out_we.start()
-    packed = [north[...], south[...]]
+    odd = odd_at("gx")
+    packed = [jnp.where(odd, even[...], other[...]), jnp.where(odd, other[...], even[...])]
     left, right, faces_phi, all_phi = solve_pair(
         NORTH, weight, own, packed, modes, couple, solved, faces, deluxe, scratch
     )
@@ -377,7 +379,7 @@
     )(links, own, far, near, modes, couple, solved, faces)
 
 
-def rows_pair(links, own, north, south, modes, couple, solved, faces, owners, of_columns):
+def rows_pair(links, own, even, other, modes, couple, solved, faces, owners, of_columns):
     return pl.pallas_call(
         rows_kernel,
         out_shape=(
@@ -392,7 +394,7 @@
         compiler_params=pltpu.CompilerParams(vmem_limit_bytes=24 << 20),
         cost_estimate=pl.CostEstimate(flops=3 << 30, bytes_accessed=4 << 20, transcendentals=0),
         name="rows_pair",
-    )(links, own, north, south, modes, couple, solved, faces, owners, *of_columns)
+    )(links, own, even, other, modes, couple, solved, faces, owners, *of_columns)
 
 
 def swap_pairs(value, axis, first):
@@ -401,12 +403,6 @@
     for low in range(first, count - 1, 2):
         pairs += [(low, low + 1), (low + 1, low)]
     return lax.ppermute(value, axis, pairs)
-
-
-def shifted(value, axis, steps):
-    count = lax.axis_size(axis)
-    initial, last = (max(0, -steps), min(count, count - steps))
-    return lax.ppermute(value, axis, [(source, source + steps) for source in range(initial, last)])
 
 
 def body(interior_inverse, coupling, face_matrix, face_modes, face_links, owner_map):
@@ -416,14 +412,14 @@
     modes = face_modes[0, 0]
     links = face_links[0, 0]
     owners = owner_map[0]
-    couple, solved, faces, own, north, south, far, near = own_blocks(inverse, couple, faces)
+    couple, solved, faces, own, even, other, far, near = own_blocks(inverse, couple, faces)
     far_part = swap_pairs(far, "gy", 1)
     near_part = swap_pairs(near, "gy", 0)
-    north_part = shifted(south, "gx", 1)
-    south_part = shifted(north, "gx", -1)
+    even_part = swap_pairs(even, "gx", 0)
+    other_part = swap_pairs(other, "gx", 1)
     of_columns = columns_pair(links, own, far_part, near_part, modes, couple, solved, faces)
     deluxe, partial = rows_pair(
-        links, own, north_part, south_part, modes, couple, solved, faces, owners, of_columns
+        links, own, even_part, other_part, modes, couple, solved, faces, owners, of_columns
     )
     count = lax.axis_size("gy")
     parts = partial.reshape(count, NCG // count, FACES * MODES)

time: 45.8 us -> 47 us (1.026)
  starting transfers between devices: 20.2 us -> 21 us
  blocking collectives: 12.5 us -> 13 us
    ppermute x2 -> x4, starting transfers between devices: 6.4 us -> 21 us  [swap_pairs(): return lax.ppermute(value, axis, pairs)]
    ppermute x2 -> x0, starting transfers between devices: 13.8 us -> none  [shifted(): lax.ppermute(value, axis, [(source, source + steps) for source in range(i...]
    all_to_all x1, blocking collectives: 12.5 us -> 13 us  [body(): coarse = lax.all_to_all(parts, 'gy', 0, 0).sum(0)]
where the time goes in v4:
time: 47 us; the launch traced here: 46.8 us
  starting transfers between devices  21 us (45%)
  blocking collectives  13 us (28%)
  Pallas kernels  11.4 us (24%)
  between operations  0.77 us (2%)
  other arithmetic  0.62 us (1%)
    ppermute x4, starting transfers between devices, swap_pairs(): return lax.ppermute(value, axis, pairs)  21 us
    all_to_all x1, blocking collectives, body(): coarse = lax.all_to_all(parts, 'gy', 0, 0).sum(0)  13 us
    pallas_call x1, Pallas kernels, own_blocks(): pl.pallas_call(own_kernel, out_shape=(jax.ShapeDtypeStruct((NI, FACES * N...  4.15 us
    pallas_call x1, Pallas kernels, rows_pair(): pl.pallas_call(rows_kernel, out_shape=(jax.ShapeDtypeStruct((FACES, NF, N...  4.13 us
    pallas_call x1, Pallas kernels, columns_pair(): pl.pallas_call(columns_kernel, out_shape=(jax.ShapeDtypeStruct((2, NF, NF...  3.13 us
  transfers between devices with their start and end apart: 4, of which 0 were waited for; matrix products, arithmetic and copies ran while one was open for 0% of the time, Pallas kernels for 7%

profile of v4, /device:TPU:9, one launch (start us, length us, event | category | flops | bytes accessed | tf_op | source)
XLA Modules:
  0.0 46.8 jit_solution(5610972275158588463)
XLA Ops:
  0.6 0.0 copy-start
  0.6 0.0 copy-start.1
  0.7 4.1 %own_blocks.1 = (bf16[768,1024]{1,0:T(8,128)(2,1)S(1)}, bf16[768,1024]{1,0:T(8,128)(2,1)S(1)}, bf16[4,256,256]{2,1,0:T(8,128)(2,1)S(1)}, f32[4,256,256]{2,1,0:T(...) custom-call(bf16[768,768]{1,0:T(8,128)(2,1)} %bitcast.16, ...), custom_call_target="tpu_custom_call" | custom-call | tf_op jit(solution)/shard_map/own_blocks/pallas_call | solution.py:127
  4.8 4.5 %collective-permute-start.2 = (f32[264,128]{1,0:T(8,128)S(1)}, f32[264,128]{1,0:T(8,128)S(1)}, u32[]{:S(2)}, u32[]{:S(2)}) collective-permute-start(f32[264,128]{1,0:T(8,128)S(1)} %get-tuple-element.23), channel_id=1, source_target_pairs={{1,2},{2,1},{3,4},{4,3},{5,6},{6,5},{7,8},{8,7},{9,10},{10,9},{11,... | collective-permute-start | bytes 405512 | tf_op jit(solution)/shard_map/ppermute | solution.py:405
  9.3 1.9 %collective-permute-start.3 = (f32[264,128]{1,0:T(8,128)S(1)}, f32[264,128]{1,0:T(8,128)S(1)}, u32[]{:S(2)}, u32[]{:S(2)}) collective-permute-start(f32[264,128]{1,0:T(8,128)S(1)} %get-tuple-element.24), channel_id=1, source_target_pairs={{0,1},{1,0},{2,3},{3,2},{4,5},{5,4},{6,7},{7,6},{8,9},{9,8},{10,11... | collective-permute-start | bytes 405512 | tf_op jit(solution)/shard_map/ppermute | solution.py:405
  11.2 3.5 %collective-permute-start = (f32[264,128]{1,0:T(8,128)S(1)}, f32[264,128]{1,0:T(8,128)S(1)}, u32[]{:S(2)}, u32[]{:S(2)}) collective-permute-start(f32[264,128]{1,0:T(8,128)S(1)} %get-tuple-element.18), channel_id=1, source_target_pairs={{0,16},{16,0},{32,48},{48,32},{64,80},{80,64},{96,112},{112,96},{1... | collective-permute-start | bytes 405512 | tf_op jit(solution)/shard_map/ppermute | solution.py:405
  14.8 11.0 %collective-permute-start.1 = (f32[264,128]{1,0:T(8,128)S(1)}, f32[264,128]{1,0:T(8,128)S(1)}, u32[]{:S(2)}, u32[]{:S(2)}) collective-permute-start(f32[264,128]{1,0:T(8,128)S(1)} %get-tuple-element.19), channel_id=1, source_target_pairs={{16,32},{32,16},{48,64},{64,48},{80,96},{96,80},{112,128},{128,112... | collective-permute-start | bytes 405512 | tf_op jit(solution)/shard_map/ppermute | solution.py:405
  25.8 0.0 collective-permute-done.2.far
  25.8 0.0 collective-permute-done.3.near
  25.8 0.0 copy-done
  25.8 0.0 copy-done.1
  25.8 0.0 copy-start.2
  25.8 3.1 %columns_pair.1 = (f32[2,256,256]{2,1,0:T(8,128)S(1)}, f32[768,128]{1,0:T(8,128)S(1)}, f32[768,128]{1,0:T(8,128)S(1)}, f32[256,128]{1,0:T(8,128)S(1)}, f32[256,128]{1,0:T(8,128)S(1)}) custom-call(s32[4]{0:T(128)S(1)} %bitcast.12, f32[4,256,256]{2,1,0:T(8,128)S(1)} %get-tuple-element.17.own, f32[264,128]{1,0:T(8,128)S(1)} %collective-permute-done.2.far, ...), custom_call_target="tpu_custom_call" | custom-call | flops 2147483648 | bytes 4194304 | tf_op jit(solution)/shard_map/columns_pair/pallas_call | solution.py:370
  29.0 0.0 collective-permute-done.even
  29.0 0.0 collective-permute-done.1.other
  29.0 0.0 copy-done.2
  29.0 4.1 %rows_pair.1 = (f32[4,256,256]{2,1,0:T(8,128)}, f32[256,128]{1,0:T(8,128)S(1)}) custom-call(s32[4]{0:T(128)S(1)} %bitcast.13, f32[4,256,256]{2,1,0:T(8,128)S(1)} %get-tuple-element.17.own, f32[264,128]{1,0:T(8,128)S(1)} %collective-permute-done.even, f32[264,128]{1,0:T(8,128)S(1)} %collective-permute-done.1.other, bf16[256,128]{1,0:T(8,128)(2,1)S(1)} %bitcast.11, ...), custom_call_target="tpu_custom_call" | custom-call | flops 3221225472 | bytes 4194304 | tf_op jit(solution)/shard_map/rows_pair/pallas_call | solution.py:383
  33.2 13.0 %all_to_all.5 = f32[16,16,128]{2,1,0:T(8,128)S(1)} all-to-all(f32[16,16,128]{2,1,0:T(8,128)S(1)} %bitcast.9), channel_id=1, replica_groups=mesh['gx'=32,'gy'=16] {'gy'}, dimensions={0} | all-to-all | bytes 262144 | tf_op jit(solution)/shard_map/all_to_all | solution.py:426
  46.2 0.6 %reduce_sum.9 = f32[16,128]{1,0:T(8,128)} reduce(f32[16,16,128]{2,1,0:T(8,128)S(1)} %all_to_all.5, f32[]{:T(128)} %constant.0.clone.1), dimensions={0}, to_apply=%region_0.0 | reduce | flops 30720 | bytes 139268 | tf_op jit(solution)/shard_map/reduce_sum | solution.py:426
Async XLA Ops:
  0.6 25.2 %copy-start = (bf16[1,1,256,128]{3,2,1,0:T(8,128)(2,1)S(1)}, bf16[1,1,256,128]{3,2,1,0:T(8,128)(2,1)}, u32[]{:S(2)}) copy-start(bf16[1,1,256,128]{3,2,1,0:T(8,128)(2,1)} %param.9) | copy-start | bytes 196612
  0.6 25.2 %copy-start.1 = (s32[1,1,4]{2,1,0:T(1,128)S(1)}, s32[1,1,4]{2,1,0:T(1,128)}, u32[]{:S(2)}) copy-start(s32[1,1,4]{2,1,0:T(1,128)} %param.10) | copy-start | bytes 52
  4.8 21.0 %collective-permute-start.2 = (f32[264,128]{1,0:T(8,128)S(1)}, f32[264,128]{1,0:T(8,128)S(1)}, u32[]{:S(2)}, u32[]{:S(2)}) collective-permute-start(f32[264,128]{1,0:T(8,128)S(1)} %get-tuple-element.23), channel_id=1, source_target_pairs={{1,2},{2,1},{3,4},{4,3},{5,6},{6,5},{7,8},{8,7},{9,10},{10,9},{11,... | collective-permute-start | bytes 405512 | tf_op jit(solution)/shard_map/ppermute | solution.py:405
  9.3 16.5 %collective-permute-start.3 = (f32[264,128]{1,0:T(8,128)S(1)}, f32[264,128]{1,0:T(8,128)S(1)}, u32[]{:S(2)}, u32[]{:S(2)}) collective-permute-start(f32[264,128]{1,0:T(8,128)S(1)} %get-tuple-element.24), channel_id=1, source_target_pairs={{0,1},{1,0},{2,3},{3,2},{4,5},{5,4},{6,7},{7,6},{8,9},{9,8},{10,11... | collective-permute-start | bytes 405512 | tf_op jit(solution)/shard_map/ppermute | solution.py:405
  11.2 17.8 %collective-permute-start = (f32[264,128]{1,0:T(8,128)S(1)}, f32[264,128]{1,0:T(8,128)S(1)}, u32[]{:S(2)}, u32[]{:S(2)}) collective-permute-start(f32[264,128]{1,0:T(8,128)S(1)} %get-tuple-element.18), channel_id=1, source_target_pairs={{0,16},{16,0},{32,48},{48,32},{64,80},{80,64},{96,112},{112,96},{1... | collective-permute-start | bytes 405512 | tf_op jit(solution)/shard_map/ppermute | solution.py:405
  14.8 14.2 %collective-permute-start.1 = (f32[264,128]{1,0:T(8,128)S(1)}, f32[264,128]{1,0:T(8,128)S(1)}, u32[]{:S(2)}, u32[]{:S(2)}) collective-permute-start(f32[264,128]{1,0:T(8,128)S(1)} %get-tuple-element.19), channel_id=1, source_target_pairs={{16,32},{32,16},{48,64},{64,48},{80,96},{96,80},{112,128},{128,112... | collective-permute-start | bytes 405512 | tf_op jit(solution)/shard_map/ppermute | solution.py:405
  25.8 3.2 %copy-start.2 = (s32[1,1,128]{2,1,0:T(1,128)S(1)}, s32[1,1,128]{2,1,0:T(1,128)}, u32[]{:S(2)}) copy-start(s32[1,1,128]{2,1,0:T(1,128)} %param.11) | copy-start | bytes 1540

commit v5 on v4

--- a/solution.py
+++ b/solution.py
@@ -49,6 +49,11 @@
 
 def odd_at(axis):
     return lax.rem(lax.axis_index(axis), 2) == 1
+
+
+def west_first():
+    low = lax.axis_index("gx") < lax.axis_size("gx") // 2
+    return odd_at("gy") == low
 
 
 def grid_iota(rows, columns, dimension):
@@ -74,7 +79,7 @@
 
 def own_kernel(
     inverse_hbm, couple_hbm, faces_hbm,
-    couple, solved, faces, own, send_even, send_odd, send_far, send_near,
+    couple, solved, faces, own, send_even, send_odd, send_first, send_last,
     inverse, sems,
 ):
     half = 2 * NF
@@ -114,7 +119,7 @@
         put(up, [jnp.where(odd, l, h) for l, h in pairs])
         put(down, [jnp.where(odd, h, l) for l, h in pairs])
 
-    put_pair(odd_at("gy"), own_of(WEST), own_of(EAST), send_near, send_far)
+    put_pair(west_first(), own_of(WEST), own_of(EAST), send_first, send_last)
     right.wait()
     solved[:, :half] = dot(inverse[...], couple[:, :half]).astype(BF16)
     put_pair(odd_at("gx"), own_of(NORTH), own_of(SOUTH), send_even, send_odd)
@@ -288,37 +293,37 @@
     )
 
 
-def columns_kernel(
-    links, own, far, near, modes, couple, solved, faces,
+def rows_kernel(
+    links, own, even, other, modes, couple, solved, faces,
     deluxe, left, right, faces_phi, all_phi,
     *scratch,
 ):
-    odd = odd_at("gy")
-    packed = [jnp.where(odd, near[...], far[...]), jnp.where(odd, far[...], near[...])]
+    odd = odd_at("gx")
+    packed = [jnp.where(odd, even[...], other[...]), jnp.where(odd, other[...], even[...])]
     left[...], right[...], faces_phi[...], all_phi[...] = solve_pair(
-        WEST, face_weights(links), own, packed, modes, couple, solved, faces, deluxe, scratch
-    )
-
-
-def rows_kernel(
-    links, own, even, other, modes, couple, solved, faces, owners,
-    deluxe_we, left_we, right_we, faces_phi_we, all_phi_we,
+        NORTH, face_weights(links), own, packed, modes, couple, solved, faces, deluxe, scratch
+    )
+
+
+def columns_kernel(
+    links, own, first, last, modes, couple, solved, faces, owners,
+    deluxe_ns, left_ns, right_ns, faces_phi_ns, all_phi_ns,
     deluxe_hbm, partial,
     deluxe, *scratch_sems,
 ):
     *scratch, sems = scratch_sems
     weight = face_weights(links)
-    out_we = pltpu.make_async_copy(deluxe_we, deluxe_hbm.at[WEST:], sems.at[1])
-    out_we.start()
-    odd = odd_at("gx")
-    packed = [jnp.where(odd, even[...], other[...]), jnp.where(odd, other[...], even[...])]
+    out_ns = pltpu.make_async_copy(deluxe_ns, deluxe_hbm.at[:WEST], sems.at[1])
+    out_ns.start()
+    from_first = west_first()
+    packed = [jnp.where(from_first, first[...], last[...]), jnp.where(from_first, last[...], first[...])]
     left, right, faces_phi, all_phi = solve_pair(
-        NORTH, weight, own, packed, modes, couple, solved, faces, deluxe, scratch
-    )
-    out = pltpu.make_async_copy(deluxe, deluxe_hbm.at[:WEST], sems.at[0])
+        WEST, weight, own, packed, modes, couple, solved, faces, deluxe, scratch
+    )
+    out = pltpu.make_async_copy(deluxe, deluxe_hbm.at[WEST:], sems.at[0])
     out.start()
-    cross = dot_three_rows(left + left_we[...], right + right_we[...])
-    own_part = dot_three_rows(all_phi + all_phi_we[...], faces_phi + faces_phi_we[...])
+    cross = dot_three_rows(left + left_ns[...], right + right_ns[...])
+    own_part = dot_three_rows(all_phi + all_phi_ns[...], faces_phi + faces_phi_ns[...])
     rows = grid_iota(FACES * MODES, FACES * MODES, 0)
     columns = grid_iota(FACES * MODES, FACES * MODES, 1)
     same = (rows // MODES) == (columns // MODES)
@@ -337,7 +342,7 @@
     high, low = split(local)
     lowest = (local - high.astype(F32) - low.astype(F32)).astype(BF16)
     partial[...] = dot(onehot, high) + (dot(onehot, low) + dot(onehot, lowest))
-    out_we.wait()
+    out_ns.wait()
     out.wait()
 
 
@@ -364,24 +369,24 @@
     ]
 
 
-def columns_pair(links, own, far, near, modes, couple, solved, faces):
+def rows_pair(links, own, even, other, modes, couple, solved, faces):
     tall = jax.ShapeDtypeStruct((NI, FACES * MODES), F32)
     short = jax.ShapeDtypeStruct((NF, FACES * MODES), F32)
     return pl.pallas_call(
-        columns_kernel,
+        rows_kernel,
         out_shape=(jax.ShapeDtypeStruct((2, NF, NF), F32), tall, tall, short, short),
         in_specs=[SMEM_SPEC] + [VMEM_SPEC] * 7,
         out_specs=(VMEM_SPEC,) * 5,
         scratch_shapes=pair_scratch(),
         compiler_params=pltpu.CompilerParams(vmem_limit_bytes=24 << 20),
         cost_estimate=pl.CostEstimate(flops=2 << 30, bytes_accessed=4 << 20, transcendentals=0),
-        name="columns_pair",
-    )(links, own, far, near, modes, couple, solved, faces)
-
-
-def rows_pair(links, own, even, other, modes, couple, solved, faces, owners, of_columns):
+        name="rows_pair",
+    )(links, own, even, other, modes, couple, solved, faces)
+
+
+def columns_pair(links, own, first, last, modes, couple, solved, faces, owners, of_rows):
     return pl.pallas_call(
-        rows_kernel,
+        columns_kernel,
         out_shape=(
             jax.ShapeDtypeStruct((FACES, NF, NF), F32),
             jax.ShapeDtypeStruct((NCG, FACES * MODES), F32),
@@ -393,16 +398,25 @@
         ],
         compiler_params=pltpu.CompilerParams(vmem_limit_bytes=24 << 20),
         cost_estimate=pl.CostEstimate(flops=3 << 30, bytes_accessed=4 << 20, transcendentals=0),
-        name="rows_pair",
-    )(links, own, even, other, modes, couple, solved, faces, owners, *of_columns)
-
-
-def swap_pairs(value, axis, first):
-    count = lax.axis_size(axis)
+        name="columns_pair",
+    )(links, own, first, last, modes, couple, solved, faces, owners, *of_rows)
+
+
+def swap_rows(value, first):
     pairs = []
-    for low in range(first, count - 1, 2):
+    for low in range(first, lax.axis_size("gx") - 1, 2):
         pairs += [(low, low + 1), (low + 1, low)]
-    return lax.ppermute(value, axis, pairs)
+    return lax.ppermute(value, "gx", pairs)
+
+
+def swap_columns(value, step):
+    rows, columns = lax.axis_size("gx"), lax.axis_size("gy")
+    pairs = []
+    for row in range(rows):
+        first = step if row < rows // 2 else 1 - step
+        for low in range(row * columns + first, (row + 1) * columns - 1, 2):
+            pairs += [(low, low + 1), (low + 1, low)]
+    return lax.ppermute(value, ("gx", "gy"), pairs)
 
 
 def body(interior_inverse, coupling, face_matrix, face_modes, face_links, owner_map):
@@ -412,14 +426,14 @@
     modes = face_modes[0, 0]
     links = face_links[0, 0]
     owners = owner_map[0]
-    couple, solved, faces, own, even, other, far, near = own_blocks(inverse, couple, faces)
-    far_part = swap_pairs(far, "gy", 1)
-    near_part = swap_pairs(near, "gy", 0)
-    even_part = swap_pairs(even, "gx", 0)
-    other_part = swap_pairs(other, "gx", 1)
-    of_columns = columns_pair(links, own, far_part, near_part, modes, couple, solved, faces)
-    deluxe, partial = rows_pair(
-        links, own, even_part, other_part, modes, couple, solved, faces, owners, of_columns
+    couple, solved, faces, own, even, other, first, last = own_blocks(inverse, couple, faces)
+    first_part = swap_columns(first, 0)
+    even_part = swap_rows(even, 0)
+    other_part = swap_rows(other, 1)
+    last_part = swap_columns(last, 1)
+    of_rows = rows_pair(links, own, even_part, other_part, modes, couple, solved, faces)
+    deluxe, partial = columns_pair(
+        links, own, first_part, last_part, modes, couple, solved, faces, owners, of_rows
     )
     count = lax.axis_size("gy")
     parts = partial.reshape(count, NCG // count, FACES * MODES)

time: 47 us -> 47.8 us (1.017)
  blocking collectives: 13 us -> 13.8 us
    all_to_all x1, blocking collectives: 13 us -> 13.8 us  [body(): coarse = lax.all_to_all(parts, 'gy', 0, 0).sum(0)]
where the time goes in v5:
time: 47.8 us; the launch traced here: 47.5 us
  starting transfers between devices  20.9 us (44%)
  blocking collectives  13.8 us (29%)
  Pallas kernels  11.4 us (24%)
  between operations  0.77 us (2%)
  other arithmetic  0.62 us (1%)
    all_to_all x1, blocking collectives, body(): coarse = lax.all_to_all(parts, 'gy', 0, 0).sum(0)  13.8 us
    ppermute x2, starting transfers between devices, swap_rows(): return lax.ppermute(value, 'gx', pairs)  13.6 us
    ppermute x2, starting transfers between devices, swap_columns(): return lax.ppermute(value, ('gx', 'gy'), pairs)  7.26 us
    pallas_call x1, Pallas kernels, own_blocks(): pl.pallas_call(own_kernel, out_shape=(jax.ShapeDtypeStruct((NI, FACES * N...  4.15 us
    pallas_call x1, Pallas kernels, columns_pair(): pl.pallas_call(columns_kernel, out_shape=(jax.ShapeDtypeStruct((FACES, NF...  4.15 us
    pallas_call x1, Pallas kernels, rows_pair(): pl.pallas_call(rows_kernel, out_shape=(jax.ShapeDtypeStruct((2, NF, NF),...  3.13 us
  transfers between devices with their start and end apart: 4, of which 0 were waited for; matrix products, arithmetic and copies ran while one was open for 0% of the time, Pallas kernels for 7%

profile of v5, /device:TPU:9, one launch (start us, length us, event | category | flops | bytes accessed | tf_op | source)
XLA Modules:
  0.0 47.5 jit_solution(11662961209737270286)
XLA Ops:
  0.6 0.0 copy-start
  0.6 0.0 copy-start.1
  0.7 4.2 %own_blocks.1 = (bf16[768,1024]{1,0:T(8,128)(2,1)S(1)}, bf16[768,1024]{1,0:T(8,128)(2,1)S(1)}, bf16[4,256,256]{2,1,0:T(8,128)(2,1)S(1)}, f32[4,256,256]{2,1,0:T(...) custom-call(bf16[768,768]{1,0:T(8,128)(2,1)} %bitcast.16, ...), custom_call_target="tpu_custom_call" | custom-call | tf_op jit(solution)/shard_map/own_blocks/pallas_call | solution.py:132
  4.8 3.5 %collective-permute-start.2 = (f32[264,128]{1,0:T(8,128)S(1)}, f32[264,128]{1,0:T(8,128)S(1)}, u32[]{:S(2)}, u32[]{:S(2)}) collective-permute-start(f32[264,128]{1,0:T(8,128)S(1)} %get-tuple-element.23), channel_id=1, source_target_pairs={{0,16},{16,0},{32,48},{48,32},{64,80},{80,64},{96,112},{112,96},{1... | collective-permute-start | bytes 405512 | tf_op jit(solution)/shard_map/ppermute | solution.py:409
  8.4 10.1 %collective-permute-start.3 = (f32[264,128]{1,0:T(8,128)S(1)}, f32[264,128]{1,0:T(8,128)S(1)}, u32[]{:S(2)}, u32[]{:S(2)}) collective-permute-start(f32[264,128]{1,0:T(8,128)S(1)} %get-tuple-element.24), channel_id=1, source_target_pairs={{16,32},{32,16},{48,64},{64,48},{80,96},{96,80},{112,128},{128,112... | collective-permute-start | bytes 405512 | tf_op jit(solution)/shard_map/ppermute | solution.py:409
  18.5 5.3 %collective-permute-start = (f32[264,128]{1,0:T(8,128)S(1)}, f32[264,128]{1,0:T(8,128)S(1)}, u32[]{:S(2)}, u32[]{:S(2)}) collective-permute-start(f32[264,128]{1,0:T(8,128)S(1)} %get-tuple-element.18), channel_id=1, source_target_pairs={{0,1},{1,0},{2,3},{3,2},{4,5},{5,4},{6,7},{7,6},{8,9},{9,8},{10,11... | collective-permute-start | bytes 405512 | tf_op jit(solution)/shard_map/ppermute | solution.py:419
  23.8 1.9 %collective-permute-start.1 = (f32[264,128]{1,0:T(8,128)S(1)}, f32[264,128]{1,0:T(8,128)S(1)}, u32[]{:S(2)}, u32[]{:S(2)}) collective-permute-start(f32[264,128]{1,0:T(8,128)S(1)} %get-tuple-element.19), channel_id=1, source_target_pairs={{1,2},{2,1},{3,4},{4,3},{5,6},{6,5},{7,8},{8,7},{9,10},{10,9},{11,... | collective-permute-start | bytes 405512 | tf_op jit(solution)/shard_map/ppermute | solution.py:419
  25.7 0.0 collective-permute-done.2.even
  25.8 0.0 collective-permute-done.3.other
  25.8 0.0 copy-done
  25.8 0.0 copy-done.1
  25.8 0.0 copy-start.2
  25.8 3.1 %rows_pair.1 = (f32[2,256,256]{2,1,0:T(8,128)S(1)}, f32[768,128]{1,0:T(8,128)S(1)}, f32[768,128]{1,0:T(8,128)S(1)}, f32[256,128]{1,0:T(8,128)S(1)}, f32[256,128]{1,0:T(8,128)S(1)}) custom-call(s32[4]{0:T(128)S(1)} %bitcast.12, f32[4,256,256]{2,1,0:T(8,128)S(1)} %get-tuple-element.17.own, f32[264,128]{1,0:T(8,128)S(1)} %collective-permute-done.2.even, ...), custom_call_target="tpu_custom_call" | custom-call | flops 2147483648 | bytes 4194304 | tf_op jit(solution)/shard_map/rows_pair/pallas_call | solution.py:375
  28.9 0.0 collective-permute-done.first
  28.9 0.0 collective-permute-done.1.last
  29.0 0.0 copy-done.2
  29.0 4.2 %columns_pair.1 = (f32[4,256,256]{2,1,0:T(8,128)}, f32[256,128]{1,0:T(8,128)S(1)}) custom-call(s32[4]{0:T(128)S(1)} %bitcast.13, f32[4,256,256]{2,1,0:T(8,128)S(1)} %get-tuple-element.17.own, f32[264,128]{1,0:T(8,128)S(1)} %collective-permute-done.first, f32[264,128]{1,0:T(8,128)S(1)} %collective-permute-done.1.last, bf16[256,128]{1,0:T(8,128)(2,1)S(1)} %bitcast.11, ...), custom_call_target="tpu_custom_call" | custom-call | flops 3221225472 | bytes 4194304 | tf_op jit(solution)/shard_map/columns_pair/pallas_call | solution.py:388
  33.1 13.8 %all_to_all.5 = f32[16,16,128]{2,1,0:T(8,128)S(1)} all-to-all(f32[16,16,128]{2,1,0:T(8,128)S(1)} %bitcast.9), channel_id=1, replica_groups=mesh['gx'=32,'gy'=16] {'gy'}, dimensions={0} | all-to-all | bytes 262144 | tf_op jit(solution)/shard_map/all_to_all | solution.py:440
  46.9 0.6 %reduce_sum.9 = f32[16,128]{1,0:T(8,128)} reduce(f32[16,16,128]{2,1,0:T(8,128)S(1)} %all_to_all.5, f32[]{:T(128)} %constant.0.clone.1), dimensions={0}, to_apply=%region_0.0 | reduce | flops 30720 | bytes 139268 | tf_op jit(solution)/shard_map/reduce_sum | solution.py:440
Async XLA Ops:
  0.6 25.1 %copy-start = (bf16[1,1,256,128]{3,2,1,0:T(8,128)(2,1)S(1)}, bf16[1,1,256,128]{3,2,1,0:T(8,128)(2,1)}, u32[]{:S(2)}) copy-start(bf16[1,1,256,128]{3,2,1,0:T(8,128)(2,1)} %param.9) | copy-start | bytes 196612
  0.6 25.1 %copy-start.1 = (s32[1,1,4]{2,1,0:T(1,128)S(1)}, s32[1,1,4]{2,1,0:T(1,128)}, u32[]{:S(2)}) copy-start(s32[1,1,4]{2,1,0:T(1,128)} %param.10) | copy-start | bytes 52
  4.8 20.9 %collective-permute-start.2 = (f32[264,128]{1,0:T(8,128)S(1)}, f32[264,128]{1,0:T(8,128)S(1)}, u32[]{:S(2)}, u32[]{:S(2)}) collective-permute-start(f32[264,128]{1,0:T(8,128)S(1)} %get-tuple-element.23), channel_id=1, source_target_pairs={{0,16},{16,0},{32,48},{48,32},{64,80},{80,64},{96,112},{112,96},{1... | collective-permute-start | bytes 405512 | tf_op jit(solution)/shard_map/ppermute | solution.py:409
  8.4 17.4 %collective-permute-start.3 = (f32[264,128]{1,0:T(8,128)S(1)}, f32[264,128]{1,0:T(8,128)S(1)}, u32[]{:S(2)}, u32[]{:S(2)}) collective-permute-start(f32[264,128]{1,0:T(8,128)S(1)} %get-tuple-element.24), channel_id=1, source_target_pairs={{16,32},{32,16},{48,64},{64,48},{80,96},{96,80},{112,128},{128,112... | collective-permute-start | bytes 405512 | tf_op jit(solution)/shard_map/ppermute | solution.py:409
  18.5 10.5 %collective-permute-start = (f32[264,128]{1,0:T(8,128)S(1)}, f32[264,128]{1,0:T(8,128)S(1)}, u32[]{:S(2)}, u32[]{:S(2)}) collective-permute-start(f32[264,128]{1,0:T(8,128)S(1)} %get-tuple-element.18), channel_id=1, source_target_pairs={{0,1},{1,0},{2,3},{3,2},{4,5},{5,4},{6,7},{7,6},{8,9},{9,8},{10,11... | collective-permute-start | bytes 405512 | tf_op jit(solution)/shard_map/ppermute | solution.py:419
  23.8 5.1 %collective-permute-start.1 = (f32[264,128]{1,0:T(8,128)S(1)}, f32[264,128]{1,0:T(8,128)S(1)}, u32[]{:S(2)}, u32[]{:S(2)}) collective-permute-start(f32[264,128]{1,0:T(8,128)S(1)} %get-tuple-element.19), channel_id=1, source_target_pairs={{1,2},{2,1},{3,4},{4,3},{5,6},{6,5},{7,8},{8,7},{9,10},{10,9},{11,... | collective-permute-start | bytes 405512 | tf_op jit(solution)/shard_map/ppermute | solution.py:419
  25.8 3.2 %copy-start.2 = (s32[1,1,128]{2,1,0:T(1,128)S(1)}, s32[1,1,128]{2,1,0:T(1,128)}, u32[]{:S(2)}) copy-start(s32[1,1,128]{2,1,0:T(1,128)} %param.11) | copy-start | bytes 1540

commit v6 on v5

--- a/solution.py
+++ b/solution.py
@@ -164,10 +164,10 @@
     return jnp.sum(rows, axis=1, keepdims=True)
 
 
-def general_solve(own, deluxe, matrix, scale, sweep, rest, power):
+def general_solve(ids, own, deluxe, matrix, scale, sweep, rest, power):
     own_norm = []
     for n in range(2):
-        m, block = matrix[n], own[n]
+        m, block = matrix[n], own[ids[n]]
         by = 1.0 / jnp.sum(jnp.where(eye(), m, 0.0), axis=1, keepdims=True)
         bound = jnp.max(jnp.sum(jnp.abs(m), axis=1, keepdims=True) * by)
         factor = jnp.where(bound < 1.75, 1.0, 1.0 / bound)
@@ -205,7 +205,7 @@
             start = sweep[n]
             total = deluxe[n] + (start + dot(left_three(power[n]), right_three(start)))
             deluxe[n] = total
-            residual = own[n] - dot(left_three(matrix[n]), right_three(total))
+            residual = own[ids[n]] - dot(left_three(matrix[n]), right_three(total))
             rest[n] = residual
             ratios.append(jnp.sum(residual * residual) / own_norm[n])
         return count + 1, now, largest(ratios)
@@ -223,14 +223,14 @@
     return [links[n].astype(F32) for n in range(FACES)]
 
 
-def solve_pair(first, weight, own, packed, modes, couple, solved, faces, deluxe, scratch):
+def solve_pair(ids, links, own, received, modes, couple, solved, faces, deluxe, scratch):
     matrix, scale, power, sweep, rest, general, phi = scratch
-    own = own.at[first : first + 2]
-    for n in range(2):
-        quarters = unpack(packed[n])
+    for n in range(2):
+        quarters = unpack(received[n][...])
+        weight = links[ids[n]].astype(F32)
         for at, quarter in enumerate(quarters):
             here = (slice((at // 2) * HALF, (at // 2 + 1) * HALF), slice((at % 2) * HALF, (at % 2 + 1) * HALF))
-            matrix[(n, *here)] = own[(n, *here)] + quarter * weight[first + n]
+            matrix[(n, *here)] = own[(ids[n], *here)] + quarter * weight
 
     norms = [[] for _ in range(2)]
     for n in range(2):
@@ -238,7 +238,7 @@
         scale[n] = jnp.broadcast_to(by, (NF, HALF))
         factor = jnp.where(eye(), 0.0, -by * matrix[n])
         norms[n].append(total_square(factor))
-        start = by * own[n]
+        start = by * own[ids[n]]
         power[0, n] = factor.astype(BF16)
         both = dot(power[0, n], jnp.concatenate([power[0, n], start.astype(BF16)], axis=1))
         square = both[:, :NF]
@@ -249,7 +249,7 @@
         start = sweep[n]
         rounded = (start + dot(power[1, n], start.astype(BF16))).astype(BF16)
         high, low = split(matrix[n])
-        residual = own[n] - (dot(high, rounded) + dot(low, rounded))
+        residual = own[ids[n]] - (dot(high, rounded) + dot(low, rounded))
         rest[n] = jnp.concatenate([scale[n]] * 2, axis=1) * residual
         rounded = rounded.astype(F32)
         norms[n].append(total_square(rounded))
@@ -268,12 +268,12 @@
 
     @pl.when(jnp.logical_not(jnp.max(largest(left_out)) < BOUND))
     def _():
-        general_solve(own, deluxe, matrix, scale, sweep, rest, general)
+        general_solve(ids, own, deluxe, matrix, scale, sweep, rest, general)
 
     face_of = grid_iota(NF, FACES * MODES, 1) // MODES
     all_phi = jnp.zeros((NF, FACES * MODES), F32)
     for n in range(2):
-        mode = jnp.where(face_of == first + n, modes[...].astype(F32), 0.0).astype(BF16)
+        mode = jnp.where(face_of == ids[n], modes[...].astype(F32), 0.0).astype(BF16)
         mapped = dot(
             jnp.concatenate(split(deluxe[n]), axis=1), jnp.concatenate([mode, mode], axis=0)
         )
@@ -284,46 +284,57 @@
         both = dot(left, phi[...])
         return both[:, : FACES * MODES] + both[:, FACES * MODES :]
 
-    columns = slice(first * NF, (first + 2) * NF)
+    def columns_of(ref):
+        return jnp.concatenate([ref[:, pl.ds(pl.multiple_of(face * NF, NF), NF)] for face in ids], axis=1)
+
     return (
-        times_phi(couple[:, columns]),
-        times_phi(solved[:, columns]),
-        times_phi(jnp.concatenate([faces[first], faces[first + 1]], axis=1)),
+        times_phi(columns_of(couple)),
+        times_phi(columns_of(solved)),
+        times_phi(jnp.concatenate([faces[face] for face in ids], axis=1)),
         all_phi,
     )
 
 
-def rows_kernel(
-    links, own, even, other, modes, couple, solved, faces,
+def early_faces():
+    return jnp.where(west_first(), WEST, EAST), jnp.where(odd_at("gx"), NORTH, SOUTH)
+
+
+def late_faces():
+    return jnp.where(west_first(), EAST, WEST), jnp.where(odd_at("gx"), SOUTH, NORTH)
+
+
+def early_kernel(
+    links, own, first, even, modes, couple, solved, faces,
     deluxe, left, right, faces_phi, all_phi,
     *scratch,
 ):
-    odd = odd_at("gx")
-    packed = [jnp.where(odd, even[...], other[...]), jnp.where(odd, other[...], even[...])]
     left[...], right[...], faces_phi[...], all_phi[...] = solve_pair(
-        NORTH, face_weights(links), own, packed, modes, couple, solved, faces, deluxe, scratch
-    )
-
-
-def columns_kernel(
-    links, own, first, last, modes, couple, solved, faces, owners,
-    deluxe_ns, left_ns, right_ns, faces_phi_ns, all_phi_ns,
+        early_faces(), links, own, (first, even), modes, couple, solved, faces, deluxe, scratch
+    )
+
+
+def late_kernel(
+    links, own, last, other, modes, couple, solved, faces, owners,
+    deluxe_early, left_early, right_early, faces_phi_early, all_phi_early,
     deluxe_hbm, partial,
     deluxe, *scratch_sems,
 ):
     *scratch, sems = scratch_sems
     weight = face_weights(links)
-    out_ns = pltpu.make_async_copy(deluxe_ns, deluxe_hbm.at[:WEST], sems.at[1])
-    out_ns.start()
-    from_first = west_first()
-    packed = [jnp.where(from_first, first[...], last[...]), jnp.where(from_first, last[...], first[...])]
+
+    def out(source, n, ids):
+        at = 2 * n if source is deluxe else 2 * n + 1
+        return pltpu.make_async_copy(source.at[n], deluxe_hbm.at[ids[n]], sems.at[at])
+
+    for n in range(2):
+        out(deluxe_early, n, early_faces()).start()
     left, right, faces_phi, all_phi = solve_pair(
-        WEST, weight, own, packed, modes, couple, solved, faces, deluxe, scratch
-    )
-    out = pltpu.make_async_copy(deluxe, deluxe_hbm.at[WEST:], sems.at[0])
-    out.start()
-    cross = dot_three_rows(left + left_ns[...], right + right_ns[...])
-    own_part = dot_three_rows(all_phi + all_phi_ns[...], faces_phi + faces_phi_ns[...])
+        late_faces(), links, own, (last, other), modes, couple, solved, faces, deluxe, scratch
+    )
+    for n in range(2):
+        out(deluxe, n, late_faces()).start()
+    cross = dot_three_rows(left + left_early[...], right + right_early[...])
+    own_part = dot_three_rows(all_phi + all_phi_early[...], faces_phi + faces_phi_early[...])
     rows = grid_iota(FACES * MODES, FACES * MODES, 0)
     columns = grid_iota(FACES * MODES, FACES * MODES, 1)
     same = (rows // MODES) == (columns // MODES)
@@ -342,8 +353,9 @@
     high, low = split(local)
     lowest = (local - high.astype(F32) - low.astype(F32)).astype(BF16)
     partial[...] = dot(onehot, high) + (dot(onehot, low) + dot(onehot, lowest))
-    out_ns.wait()
-    out.wait()
+    for n in range(2):
+        out(deluxe_early, n, early_faces()).wait()
+        out(deluxe, n, late_faces()).wait()
 
 
 def dot_three_rows(one, two):
@@ -369,24 +381,24 @@
     ]
 
 
-def rows_pair(links, own, even, other, modes, couple, solved, faces):
+def early_pair(links, own, first, even, modes, couple, solved, faces):
     tall = jax.ShapeDtypeStruct((NI, FACES * MODES), F32)
     short = jax.ShapeDtypeStruct((NF, FACES * MODES), F32)
     return pl.pallas_call(
-        rows_kernel,
+        early_kernel,
         out_shape=(jax.ShapeDtypeStruct((2, NF, NF), F32), tall, tall, short, short),
         in_specs=[SMEM_SPEC] + [VMEM_SPEC] * 7,
         out_specs=(VMEM_SPEC,) * 5,
         scratch_shapes=pair_scratch(),
         compiler_params=pltpu.CompilerParams(vmem_limit_bytes=24 << 20),
         cost_estimate=pl.CostEstimate(flops=2 << 30, bytes_accessed=4 << 20, transcendentals=0),
-        name="rows_pair",
-    )(links, own, even, other, modes, couple, solved, faces)
-
-
-def columns_pair(links, own, first, last, modes, couple, solved, faces, owners, of_rows):
+        name="early_pair",
+    )(links, own, first, even, modes, couple, solved, faces)
+
+
+def late_pair(links, own, last, other, modes, couple, solved, faces, owners, early):
     return pl.pallas_call(
-        columns_kernel,
+        late_kernel,
         out_shape=(
             jax.ShapeDtypeStruct((FACES, NF, NF), F32),
             jax.ShapeDtypeStruct((NCG, FACES * MODES), F32),
@@ -394,12 +406,12 @@
         in_specs=[SMEM_SPEC] + [VMEM_SPEC] * 13,
         out_specs=(pl.BlockSpec(memory_space=pltpu.HBM), VMEM_SPEC),
         scratch_shapes=[
-            pltpu.VMEM((2, NF, NF), F32), *pair_scratch(), pltpu.SemaphoreType.DMA((2,)),
+            pltpu.VMEM((2, NF, NF), F32), *pair_scratch(), pltpu.SemaphoreType.DMA((4,)),
         ],
         compiler_params=pltpu.CompilerParams(vmem_limit_bytes=24 << 20),
         cost_estimate=pl.CostEstimate(flops=3 << 30, bytes_accessed=4 << 20, transcendentals=0),
-        name="columns_pair",
-    )(links, own, first, last, modes, couple, solved, faces, owners, *of_rows)
+        name="late_pair",
+    )(links, own, last, other, modes, couple, solved, faces, owners, *early)
 
 
 def swap_rows(value, first):
@@ -431,9 +443,9 @@
     even_part = swap_rows(even, 0)
     other_part = swap_rows(other, 1)
     last_part = swap_columns(last, 1)
-    of_rows = rows_pair(links, own, even_part, other_part, modes, couple, solved, faces)
-    deluxe, partial = columns_pair(
-        links, own, first_part, last_part, modes, couple, solved, faces, owners, of_rows
+    early = early_pair(links, own, first_part, even_part, modes, couple, solved, faces)
+    deluxe, partial = late_pair(
+        links, own, last_part, other_part, modes, couple, solved, faces, owners, early
     )
     count = lax.axis_size("gy")
     parts = partial.reshape(count, NCG // count, FACES * MODES)

time: 47.8 us -> 47.4 us (level)
  blocking collectives: 13.8 us -> 13.1 us
    ppermute x2, starting transfers between devices: 13.6 us -> 14.8 us  [swap_rows(): return lax.ppermute(value, 'gx', pairs)]
    ppermute x2, starting transfers between devices: 7.26 us -> 6.4 us  [swap_columns(): return lax.ppermute(value, ('gx', 'gy'), pairs)]
    all_to_all x1, blocking collectives: 13.8 us -> 13.1 us  [body(): coarse = lax.all_to_all(parts, 'gy', 0, 0).sum(0)]
where the time goes in v6:
time: 47.4 us; the launch traced here: 47.1 us
  starting transfers between devices  21.2 us (45%)
  blocking collectives  13.1 us (28%)
  Pallas kernels  11.4 us (24%)
  between operations  0.77 us (2%)
  other arithmetic  0.62 us (1%)
    ppermute x2, starting transfers between devices, swap_rows(): return lax.ppermute(value, 'gx', pairs)  14.8 us
    all_to_all x1, blocking collectives, body(): coarse = lax.all_to_all(parts, 'gy', 0, 0).sum(0)  13.1 us
    ppermute x2, starting transfers between devices, swap_columns(): return lax.ppermute(value, ('gx', 'gy'), pairs)  6.4 us
    pallas_call x1, Pallas kernels, late_pair(): pl.pallas_call(late_kernel, out_shape=(jax.ShapeDtypeStruct((FACES, NF, N...  4.17 us
    pallas_call x1, Pallas kernels, own_blocks(): pl.pallas_call(own_kernel, out_shape=(jax.ShapeDtypeStruct((NI, FACES * N...  4.15 us
    pallas_call x1, Pallas kernels, early_pair(): pl.pallas_call(early_kernel, out_shape=(jax.ShapeDtypeStruct((2, NF, NF),...  3.11 us
  transfers between devices with their start and end apart: 4, of which 0 were waited for; matrix products, arithmetic and copies ran while one was open for 0% of the time, Pallas kernels for 7%

profile of v6, /device:TPU:9, one launch (start us, length us, event | category | flops | bytes accessed | tf_op | source)
XLA Modules:
  0.0 47.1 jit_solution(14253690230850532464)
XLA Ops:
  0.6 0.0 copy-start
  0.6 0.0 copy-start.1
  0.7 4.2 %own_blocks.1 = (bf16[768,1024]{1,0:T(8,128)(2,1)S(1)}, bf16[768,1024]{1,0:T(8,128)(2,1)S(1)}, bf16[4,256,256]{2,1,0:T(8,128)(2,1)S(1)}, f32[4,256,256]{2,1,0:T(...) custom-call(bf16[768,768]{1,0:T(8,128)(2,1)} %bitcast.16, ...), custom_call_target="tpu_custom_call" | custom-call | tf_op jit(solution)/shard_map/own_blocks/pallas_call | solution.py:132
  4.8 4.5 %collective-permute-start.2 = (f32[264,128]{1,0:T(8,128)S(1)}, f32[264,128]{1,0:T(8,128)S(1)}, u32[]{:S(2)}, u32[]{:S(2)}) collective-permute-start(f32[264,128]{1,0:T(8,128)S(1)} %get-tuple-element.23), channel_id=1, source_target_pairs={{0,1},{1,0},{2,3},{3,2},{4,5},{5,4},{6,7},{7,6},{8,9},{9,8},{10,11... | collective-permute-start | bytes 405512 | tf_op jit(solution)/shard_map/ppermute | solution.py:431
  9.3 3.5 %collective-permute-start.3 = (f32[264,128]{1,0:T(8,128)S(1)}, f32[264,128]{1,0:T(8,128)S(1)}, u32[]{:S(2)}, u32[]{:S(2)}) collective-permute-start(f32[264,128]{1,0:T(8,128)S(1)} %get-tuple-element.24), channel_id=1, source_target_pairs={{0,16},{16,0},{32,48},{48,32},{64,80},{80,64},{96,112},{112,96},{1... | collective-permute-start | bytes 405512 | tf_op jit(solution)/shard_map/ppermute | solution.py:421
  12.9 1.9 %collective-permute-start = (f32[264,128]{1,0:T(8,128)S(1)}, f32[264,128]{1,0:T(8,128)S(1)}, u32[]{:S(2)}, u32[]{:S(2)}) collective-permute-start(f32[264,128]{1,0:T(8,128)S(1)} %get-tuple-element.18), channel_id=1, source_target_pairs={{1,2},{2,1},{3,4},{4,3},{5,6},{6,5},{7,8},{8,7},{9,10},{10,9},{11,... | collective-permute-start | bytes 405512 | tf_op jit(solution)/shard_map/ppermute | solution.py:431
  14.8 11.3 %collective-permute-start.1 = (f32[264,128]{1,0:T(8,128)S(1)}, f32[264,128]{1,0:T(8,128)S(1)}, u32[]{:S(2)}, u32[]{:S(2)}) collective-permute-start(f32[264,128]{1,0:T(8,128)S(1)} %get-tuple-element.19), channel_id=1, source_target_pairs={{16,32},{32,16},{48,64},{64,48},{80,96},{96,80},{112,128},{128,112... | collective-permute-start | bytes 405512 | tf_op jit(solution)/shard_map/ppermute | solution.py:421
  26.1 0.0 collective-permute-done.2.first
  26.1 0.0 collective-permute-done.3.even
  26.1 0.0 copy-done
  26.1 0.0 copy-done.1
  26.1 0.0 copy-start.2
  26.1 3.1 %early_pair.1 = (f32[2,256,256]{2,1,0:T(8,128)S(1)}, f32[768,128]{1,0:T(8,128)S(1)}, f32[768,128]{1,0:T(8,128)S(1)}, f32[256,128]{1,0:T(8,128)S(1)}, f32[256,128]{1,0:T(8,128)S(1)}) custom-call(s32[4]{0:T(128)S(1)} %bitcast.12, f32[4,256,256]{2,1,0:T(8,128)S(1)} %get-tuple-element.17.own, f32[264,128]{1,0:T(8,128)S(1)} %collective-permute-done.2.first, ...), custom_call_target="tpu_custom_call" | custom-call | flops 2147483648 | bytes 4194304 | tf_op jit(solution)/shard_map/early_pair/pallas_call | solution.py:387
  29.2 0.0 collective-permute-done.last
  29.3 0.0 collective-permute-done.1.other
  29.3 0.0 copy-done.2
  29.3 4.2 %late_pair.1 = (f32[4,256,256]{2,1,0:T(8,128)}, f32[256,128]{1,0:T(8,128)S(1)}) custom-call(s32[4]{0:T(128)S(1)} %bitcast.13, f32[4,256,256]{2,1,0:T(8,128)S(1)} %get-tuple-element.17.own, f32[264,128]{1,0:T(8,128)S(1)} %collective-permute-done.last, f32[264,128]{1,0:T(8,128)S(1)} %collective-permute-done.1.other, bf16[256,128]{1,0:T(8,128)(2,1)S(1)} %bitcast.11, ...), custom_call_target="tpu_custom_call" | custom-call | flops 3221225472 | bytes 4194304 | tf_op jit(solution)/shard_map/late_pair/pallas_call | solution.py:400
  33.5 13.1 %all_to_all.5 = f32[16,16,128]{2,1,0:T(8,128)S(1)} all-to-all(f32[16,16,128]{2,1,0:T(8,128)S(1)} %bitcast.9), channel_id=1, replica_groups=mesh['gx'=32,'gy'=16] {'gy'}, dimensions={0} | all-to-all | bytes 262144 | tf_op jit(solution)/shard_map/all_to_all | solution.py:452
  46.5 0.6 %reduce_sum.9 = f32[16,128]{1,0:T(8,128)} reduce(f32[16,16,128]{2,1,0:T(8,128)S(1)} %all_to_all.5, f32[]{:T(128)} %constant.0.clone.1), dimensions={0}, to_apply=%region_0.0 | reduce | flops 30720 | bytes 139268 | tf_op jit(solution)/shard_map/reduce_sum | solution.py:452
Async XLA Ops:
  0.6 25.5 %copy-start = (bf16[1,1,256,128]{3,2,1,0:T(8,128)(2,1)S(1)}, bf16[1,1,256,128]{3,2,1,0:T(8,128)(2,1)}, u32[]{:S(2)}) copy-start(bf16[1,1,256,128]{3,2,1,0:T(8,128)(2,1)} %param.9) | copy-start | bytes 196612
  0.6 25.5 %copy-start.1 = (s32[1,1,4]{2,1,0:T(1,128)S(1)}, s32[1,1,4]{2,1,0:T(1,128)}, u32[]{:S(2)}) copy-start(s32[1,1,4]{2,1,0:T(1,128)} %param.10) | copy-start | bytes 52
  4.8 21.3 %collective-permute-start.2 = (f32[264,128]{1,0:T(8,128)S(1)}, f32[264,128]{1,0:T(8,128)S(1)}, u32[]{:S(2)}, u32[]{:S(2)}) collective-permute-start(f32[264,128]{1,0:T(8,128)S(1)} %get-tuple-element.23), channel_id=1, source_target_pairs={{0,1},{1,0},{2,3},{3,2},{4,5},{5,4},{6,7},{7,6},{8,9},{9,8},{10,11... | collective-permute-start | bytes 405512 | tf_op jit(solution)/shard_map/ppermute | solution.py:431
  9.3 16.8 %collective-permute-start.3 = (f32[264,128]{1,0:T(8,128)S(1)}, f32[264,128]{1,0:T(8,128)S(1)}, u32[]{:S(2)}, u32[]{:S(2)}) collective-permute-start(f32[264,128]{1,0:T(8,128)S(1)} %get-tuple-element.24), channel_id=1, source_target_pairs={{0,16},{16,0},{32,48},{48,32},{64,80},{80,64},{96,112},{112,96},{1... | collective-permute-start | bytes 405512 | tf_op jit(solution)/shard_map/ppermute | solution.py:421
  12.9 16.4 %collective-permute-start = (f32[264,128]{1,0:T(8,128)S(1)}, f32[264,128]{1,0:T(8,128)S(1)}, u32[]{:S(2)}, u32[]{:S(2)}) collective-permute-start(f32[264,128]{1,0:T(8,128)S(1)} %get-tuple-element.18), channel_id=1, source_target_pairs={{1,2},{2,1},{3,4},{4,3},{5,6},{6,5},{7,8},{8,7},{9,10},{10,9},{11,... | collective-permute-start | bytes 405512 | tf_op jit(solution)/shard_map/ppermute | solution.py:431
  14.8 14.5 %collective-permute-start.1 = (f32[264,128]{1,0:T(8,128)S(1)}, f32[264,128]{1,0:T(8,128)S(1)}, u32[]{:S(2)}, u32[]{:S(2)}) collective-permute-start(f32[264,128]{1,0:T(8,128)S(1)} %get-tuple-element.19), channel_id=1, source_target_pairs={{16,32},{32,16},{48,64},{64,48},{80,96},{96,80},{112,128},{128,112... | collective-permute-start | bytes 405512 | tf_op jit(solution)/shard_map/ppermute | solution.py:421
  26.1 3.2 %copy-start.2 = (s32[1,1,128]{2,1,0:T(1,128)S(1)}, s32[1,1,128]{2,1,0:T(1,128)}, u32[]{:S(2)}) copy-start(s32[1,1,128]{2,1,0:T(1,128)} %param.11) | copy-start | bytes 1540
